TPU v7x, 128 devices: a whole 4x4x4 slice. The times are simulated.
128 devices in a mesh: lon: 32 (over z, x, y_hi), lat: 4 (over y_lo, core).
Axes of the slice: x: 4, y: 4 (y_hi: 2, y_lo: 2; y = y_hi * 2 + y_lo), z: 4, core: 2. Of those that a mesh axis runs over, the one named last changes fastest.
Arguments:
- ocean_state: float32 [4, 3, 512, 8192], P(None, None, 'lat', 'lon'), may hold values from -6 to 6
- mixing: float32 [3, 512, 8192], P(None, 'lat', 'lon'), may hold values from 0.1 to 1
- land_sea: int32 [512, 8192], P('lat', 'lon'), may hold values 0 or 1
Outputs:
- final_state: float32 [4, 3, 512, 8192], P(None, None, 'lat', 'lon')
All inputs are finite; a program needn't handle non-finite values. No bound on the sum of `land_sea` on one device may be relied on, other than what follows from the above.
Results may differ from a plain program's by a relative error of at most 0.000029.
Values sent between devices are 32-bit elements; how exact they have to be, the bound alone decides.
No kernel may reach another device: no remote copies, remote signals or barrier semaphores. Data moves between devices by JAX's collectives and lax.ppermute only.
A program may use at most 128 MiB of HBM per device.

v0:
```python
import functools
import jax
import jax.numpy as jnp
from jax import lax
from jax.experimental import pallas as pl
from jax.experimental.pallas import tpu as pltpu
from jax.sharding import PartitionSpec as P

STEPS = 8
K = 3
HALO = 2 * STEPS
LANES = 128
PAD = 8

THERMAL = 0.2
HALINE = 0.15
GRAVITY = 0.5
TIMESTEP = 0.1

STATE = 4 * K
PLANES = STATE + K + 1
VMEM_LIMIT = 48 * 1024 * 1024
SPANS = (21, 19, 19, 19, 19, 17, 17, 17)


def params():
    return pltpu.CompilerParams(vmem_limit_bytes=VMEM_LIMIT)


def shifted(x, by):
    return pltpu.roll(x, by % LANES, 1)


def pack_rows_kernel(xl, xh, ml, mh, wl, wh, to_a, to_b):
    even = lax.rem(lax.axis_index("lat"), 2) == 0

    def fill(dest, x, m, w):
        dest[:STATE] = x[...]
        dest[STATE : STATE + K] = m[...]
        dest[STATE + K] = TIMESTEP * w[...].astype(jnp.float32)

    @pl.when(even)
    def _():
        fill(to_b, xh, mh, wh)
        fill(to_a, xl, ml, wl)

    @pl.when(jnp.logical_not(even))
    def _():
        fill(to_b, xl, ml, wl)
        fill(to_a, xh, mh, wh)


def pack_rows(x, mixing, land):
    rows, cols = land.shape
    last = rows // HALO - 1
    specs = []
    for lead in ((STATE,), (K,), ()):
        for at in (0, last):
            specs.append(pl.BlockSpec(lead + (HALO, cols), functools.partial(lambda at, n, g: (0,) * n + (at, 0), at, len(lead))))
    slab = jax.ShapeDtypeStruct((PLANES, HALO, cols), jnp.float32)
    return pl.pallas_call(
        pack_rows_kernel,
        grid=(1,),
        in_specs=specs,
        out_specs=[pl.BlockSpec(slab.shape, lambda g: (0, 0, 0))] * 2,
        out_shape=[slab, slab],
        compiler_params=params(),
        name="pack_rows",
    )(x, x, mixing, mixing, land, land)


def fold(slab):
    planes, rows, cols = slab.shape
    flat = slab.reshape(planes * rows, cols)
    n = planes * rows
    i = lax.broadcasted_iota(jnp.int32, (n, n), 0)
    j = lax.broadcasted_iota(jnp.int32, (n, n), 1)
    plane = i // rows
    sign = jnp.where(jnp.logical_and(plane >= 2 * K, plane < STATE), -1.0, 1.0)
    left = jnp.where(j == plane * rows + (rows - 1 - (i - plane * rows)), sign, 0.0).astype(jnp.float32)
    a = lax.broadcasted_iota(jnp.int32, (cols, cols), 0)
    b = lax.broadcasted_iota(jnp.int32, (cols, cols), 1)
    right = jnp.where(a + b == cols - 1, 1.0, 0.0).astype(jnp.float32)
    dot = functools.partial(jnp.dot, precision=lax.Precision.HIGHEST, preferred_element_type=jnp.float32)
    return dot(dot(left, flat), right).reshape(slab.shape)


def extend_kernel(x, m, w, ra, rb, tiles, send_low, send_high, cor, south, north):
    lat = lax.axis_index("lat")
    even = lax.rem(lat, 2) == 0
    block = x.shape[1]
    total = block * lax.axis_size("lat")

    @pl.when(even)
    def _():
        north[...] = rb[...]
        south[...] = ra[...]

    @pl.when(jnp.logical_not(even))
    def _():
        south[...] = rb[...]

        @pl.when(lat == lax.axis_size("lat") - 1)
        def _():
            north[...] = fold(ra[...])

        @pl.when(lat != lax.axis_size("lat") - 1)
        def _():
            north[...] = ra[...]

    row = lax.broadcasted_iota(jnp.int32, cor.shape, 0) + (lat * block - HALO - PAD)
    cor[...] = jnp.sin(jnp.pi * (row.astype(jnp.float32) + 0.5) / total - jnp.pi / 2)

    def put(at, planes, low, high, rows):
        lane = lax.broadcasted_iota(jnp.int32, (rows, LANES), 1)
        packs = []
        for p, lo, hi in zip(planes, low, high):
            here = pl.ds(at, rows)
            tiles[0, p, here] = lo
            tiles[1, p, here] = jnp.where(lane < 32, shifted(lo, -96), shifted(hi, 32))
            edge = jnp.where(lane < 48, shifted(lo, 16), shifted(hi, -16))
            tiles[2, p, here] = edge
            packs.append((lo, hi))
        return packs

    def rows_at(at, source, rows):
        lane = lax.broadcasted_iota(jnp.int32, (rows, LANES), 1)
        for group in range(PLANES // 8):
            low = jnp.zeros((rows, LANES), jnp.float32)
            high = jnp.zeros((rows, LANES), jnp.float32)
            for q in range(8):
                p = group * 8 + q
                lo, hi = source(p)
                put(PAD + at, [p], [lo], [hi], rows)
                mine = jnp.logical_and(lane >= 16 * q, lane < 16 * q + 16)
                low = jnp.where(mine, shifted(lo, 16 * q), low)
                high = jnp.where(mine, shifted(hi, 16 * q - 112), high)
            send_low[group, pl.ds(at, rows)] = low
            send_high[group, pl.ds(at, rows)] = high

    def from_slab(ref, r):
        def source(p):
            return ref[p, pl.ds(r, 8), :LANES], ref[p, pl.ds(r, 8), LANES:]
        return source

    for r in range(0, HALO, 8):
        rows_at(r, from_slab(south, r), 8)
        rows_at(HALO + block + r, from_slab(north, r), 8)

    @pl.loop(0, block // 8)
    def _(g):
        r = pl.multiple_of(g * 8, 8)

        def source(p):
            if p < STATE:
                return x[p, pl.ds(r, 8), :LANES], x[p, pl.ds(r, 8), LANES:]
            if p < STATE + K:
                return m[p - STATE, pl.ds(r, 8), :LANES], m[p - STATE, pl.ds(r, 8), LANES:]
            return (
                TIMESTEP * w[pl.ds(r, 8), :LANES].astype(jnp.float32),
                TIMESTEP * w[pl.ds(r, 8), LANES:].astype(jnp.float32),
            )

        rows_at(HALO + r, source, 8)


def extend(x, mixing, land, ra, rb):
    block, cols = land.shape
    span = block + 2 * HALO
    f32 = jnp.float32
    vmem = pl.BlockSpec(memory_space=pltpu.VMEM)
    return pl.pallas_call(
        extend_kernel,
        in_specs=[vmem] * 5,
        out_specs=[vmem] * 4,
        out_shape=[
            jax.ShapeDtypeStruct((3, PLANES, span + 2 * PAD, LANES), f32),
            jax.ShapeDtypeStruct((PLANES // 8, span, LANES), f32),
            jax.ShapeDtypeStruct((PLANES // 8, span, LANES), f32),
            jax.ShapeDtypeStruct((span + 2 * PAD, LANES), f32),
        ],
        scratch_shapes=[pltpu.VMEM((PLANES, HALO, cols), f32)] * 2,
        compiler_params=params(),
        name="extend",
    )(x, mixing, land, ra, rb)


def substep(src, dst, coef, cor, start, dst_start, span, unroll=1):
    def load(ref, p, t):
        return ref[p, pl.ds(start + t, 8, stride=span), :]

    def face(prev, here, nxt, nxt2):
        a = here + nxt
        return a, 7.0 * a - (prev + nxt2)

    def density(t, k):
        return -0.25 * THERMAL * load(src, k, t) + 0.25 * HALINE * load(src, K + k, t)

    def pressures(t):
        out = [density(t, 0)]
        for k in range(1, K):
            out.append(out[-1] + density(t, k))
        return out

    def fluxes(t):
        out = [None] * STATE
        for k in range(K):
            order = [3, 0, 1, 2]
            speed = None
            for f in order:
                p = f * K + k
                a, value = face(load(src, p, t - 1), load(src, p, t), load(src, p, t + 1), load(src, p, t + 2))
                if f == 3:
                    speed = a
                out[p] = speed * value
        return out

    def row(t, carry):
        below_flux, p_prev, p_here = carry
        wet = coef(15)(t)
        wet24 = wet * (1.0 / 24.0)
        wet_cor = wet * cor[pl.ds(start + t, 8, stride=span), :]
        p_next = pressures(t + 1)
        above = fluxes(t)
        for k in range(K):
            wet_mix = wet * coef(STATE + k)(t)
            speed = None
            for f in (2, 3, 0, 1):
                p = f * K + k
                q = load(src, p, t)
                east = shifted(q, -1)
                west = shifted(q, 1)
                a, value = face(west, q, east, shifted(q, -2))
                if f == 2:
                    speed = a
                flux = speed * value
                adv = (flux - shifted(flux, 1)) + (above[p] - below_flux[p])
                lap = (east + west) + (load(src, p, t + 1) + load(src, p, t - 1))
                if f < 2:
                    if 0 < k < K - 1:
                        lap = lap + 0.5 * (load(src, p - 1, t) + load(src, p + 1, t)) - 5.0 * q
                    elif k == 0:
                        lap = lap + 0.5 * load(src, p + 1, t) - 4.5 * q
                    else:
                        lap = lap + 0.5 * load(src, p - 1, t) - 4.5 * q
                else:
                    lap = lap - 4.0 * q
                new = q + (wet_mix * lap - wet24 * adv)
                if f == 2:
                    grad = shifted(p_here[k], -1) - shifted(p_here[k], 1)
                    new = new + (wet_cor * load(src, p + K, t) - wet * grad)
                if f == 3:
                    grad = p_next[k] - p_prev[k]
                    new = new - (wet_cor * load(src, p - K, t) + wet * grad)
                dst[p, pl.ds(dst_start + t, 8, stride=span), :] = new
        return above, p_here, p_next

    init = (fluxes(-1), pressures(-1), pressures(0))
    lax.fori_loop(0, span, row, init, unroll=unroll)


def window(tile, cor, even, odd, out):
    span_rows = tile.shape[1] - 2 * PAD
    src = tile
    for s in range(STEPS):
        span = SPANS[s]
        need = span_rows - 4 * (s + 1)
        spare = (8 * span - need) // 2
        start = PAD + 2 * (s + 1) - spare
        dst = out if s == STEPS - 1 else (even if s % 2 == 0 else odd)
        dst_start = PAD - spare if s == STEPS - 1 else start

        def coef(p, start=start, span=span):
            return lambda t: tile[p, pl.ds(start + t, 8, stride=span), :]

        substep(src, dst, coef, cor, start, dst_start, span)
        src = dst


def interior_kernel(tiles, cor, out, even, odd):
    @pl.loop(0, 2)
    def _(i):
        window(tiles.at[i], cor, even, odd, out.at[i])


def interior(tiles, cor):
    rows = tiles.shape[2]
    block = rows - 2 * PAD - 2 * HALO
    vmem = pl.BlockSpec(memory_space=pltpu.VMEM)
    cells = 2 * STATE * rows * LANES
    return pl.pallas_call(
        interior_kernel,
        in_specs=[pl.BlockSpec((2,) + tiles.shape[1:], lambda g: (0, 0, 0, 0)), pl.BlockSpec(cor.shape, lambda g: (0, 0))],
        out_specs=pl.BlockSpec((2, STATE, block + 2 * PAD, LANES), lambda g: (0, 0, 0, 0)),
        grid=(1,),
        out_shape=jax.ShapeDtypeStruct((2, STATE, block + 2 * PAD, LANES), jnp.float32),
        scratch_shapes=[pltpu.VMEM((STATE, rows, LANES), jnp.float32)] * 2,
        compiler_params=params(),
        cost_estimate=pl.CostEstimate(flops=STEPS * 30 * cells, transcendentals=0, bytes_accessed=8 * cells),
        name="interior",
    )(tiles, cor)


def edge_kernel(tiles, cor, got_low, got_high, inner, out, tile, even, odd, edge):
    span = got_low.shape[1]
    block = out.shape[1]

    @pl.loop(0, span // 8)
    def _(g):
        r = pl.multiple_of(g * 8, 8)
        lane = lax.broadcasted_iota(jnp.int32, (8, LANES), 1)
        for p in range(PLANES):
            left = shifted(got_low[p // 8, pl.ds(r, 8)], -16 * (p % 8))
            right = shifted(got_high[p // 8, pl.ds(r, 8)], 112 - 16 * (p % 8))
            mid = tiles[0, p, pl.ds(PAD + r, 8)]
            tile[p, pl.ds(PAD + r, 8)] = jnp.where(lane < 16, left, jnp.where(lane >= 112, right, mid))

    window(tile, cor, even, odd, edge)

    @pl.loop(0, block // 8)
    def _(g):
        r = pl.multiple_of(g * 8, 8)
        lane = lax.broadcasted_iota(jnp.int32, (8, LANES), 1)
        for p in range(STATE):
            here = pl.ds(PAD + r, 8)
            e = edge[p, here]
            lo = inner[0, p, here]
            hi = inner[1, p, here]
            out[p, pl.ds(r, 8), :LANES] = jnp.where(lane < 16, shifted(e, -16), jnp.where(lane < 112, lo, shifted(hi, 96)))
            out[p, pl.ds(r, 8), LANES:] = jnp.where(lane < 80, shifted(hi, -32), shifted(e, 16))


def edges(tiles, cor, got_low, got_high, inner, cols):
    rows = tiles.shape[2]
    block = rows - 2 * PAD - 2 * HALO
    whole = lambda a: pl.BlockSpec(a.shape, functools.partial(lambda n, g: (0,) * n, len(a.shape)))
    f32 = jnp.float32
    shape = jax.ShapeDtypeStruct((STATE, block, cols), f32)
    return pl.pallas_call(
        edge_kernel,
        grid=(1,),
        in_specs=[pl.BlockSpec((1,) + tiles.shape[1:], lambda g: (2, 0, 0, 0)), whole(cor), whole(got_low), whole(got_high), whole(inner)],
        out_specs=whole(shape),
        out_shape=shape,
        scratch_shapes=[
            pltpu.VMEM((PLANES, rows, LANES), f32),
            pltpu.VMEM((STATE, rows, LANES), f32),
            pltpu.VMEM((STATE, rows, LANES), f32),
            pltpu.VMEM((STATE, block + 2 * PAD, LANES), f32),
        ],
        compiler_params=params(),
        name="edges",
    )(tiles, cor, got_low, got_high, inner)


def body(ocean_state, mixing, land_sea):
    block, cols = land_sea.shape
    n_lon, n_lat = lax.axis_size("lon"), lax.axis_size("lat")
    axes = ("lon", "lat")

    def at(i, l):
        return (i % n_lon) * n_lat + l

    pairs_b = [(at(i, l), at(i, l ^ 1)) for i in range(n_lon) for l in range(n_lat)]
    pairs_a = []
    for i in range(n_lon):
        for l in range(1, n_lat - 1, 2):
            pairs_a += [(at(i, l), at(i, l + 1)), (at(i, l + 1), at(i, l))]
        pairs_a.append((at(i, n_lat - 1), at(n_lon - 1 - i, n_lat - 1)))
    east = [(i, (i + 1) % n_lon) for i in range(n_lon)]
    west = [((i + 1) % n_lon, i) for i in range(n_lon)]

    x = ocean_state.reshape(STATE, block, cols)
    to_a, to_b = pack_rows(x, mixing, land_sea)
    ra = lax.ppermute(to_a, axes, pairs_a)
    rb = lax.ppermute(to_b, axes, pairs_b)
    tiles, send_low, send_high, cor = extend(x, mixing, land_sea, ra, rb)
    got_low = lax.ppermute(send_high, "lon", east)
    got_high = lax.ppermute(send_low, "lon", west)
    inner = interior(tiles, cor)
    out = edges(tiles, cor, got_low, got_high, inner, cols)
    return out.reshape(ocean_state.shape)


def solution(mesh):
    in_specs = (P(None, None, "lat", "lon"), P(None, "lat", "lon"), P("lat", "lon"))
    out_specs = P(None, None, "lat", "lon")
    return jax.shard_map(body, mesh=mesh, in_specs=in_specs, out_specs=out_specs, check_vma=False)
```

profile of v0, /device:TPU:9, one launch (start us, length us, event | category | flops | bytes accessed | tf_op | source)
XLA Modules:
  0.0 119.7 jit_solution(3855312985282917665)
XLA Ops:
  0.0 0.0 copy-start.1
  0.0 1.4 %copy-done.1 = f32[4,3,128,256]{3,2,1,0:T(8,128)S(1)} copy-done((f32[4,3,128,256]{3,2,1,0:T(8,128)S(1)}, f32[4,3,128,256]{3,2,1,0:T(8,128)}, u32[]{:S(2)}) %copy-start.1) | copy-done | bytes 1572888
  1.4 0.0 copy-start.2
  1.4 1.0 copy-done.2
  2.4 0.0 copy-start.3
  2.4 0.9 copy-done.3
  3.3 0.1 pack_rows.1
  3.4 9.6 %collective-permute-start = (f32[16,16,256]{2,1,0:T(8,128)S(1)}, f32[16,16,256]{2,1,0:T(8,128)S(1)}, u32[]{:S(2)}, u32[]{:S(2)}) collective-permute-start(f32[16,16,256]{2,1,0:T(8,128)S(1)} %get-tuple-element.11), channel_id=1, source_target_pairs={{1,2},{2,1},{3,127},{5,6},{6,5},{7,123},{9,10},{10,9},{11,119},{13... | collective-permute-start | bytes 786440 | tf_op jit(solution)/shard_map/ppermute | solution.py:375
  13.0 0.1 collective-permute-start.1
  13.1 3.8 %collective-permute-done.ra = f32[16,16,256]{2,1,0:T(8,128)S(1)} collective-permute-done((f32[16,16,256]{2,1,0:T(8,128)S(1)}, f32[16,16,256]{2,1,0:T(8,128)S(1)}, u32[]{:S(2)}, u32[]{:S(2)}) %collective-permute-start) | collective-permute-done | bytes 262176 | tf_op jit(solution)/shard_map/ppermute | solution.py:375
  16.8 0.0 collective-permute-done.1.rb
  16.8 6.2 %extend.1 = (f32[3,16,176,128]{3,2,1,0:T(8,128)}, f32[2,160,128]{2,1,0:T(8,128)S(1)}, f32[2,160,128]{2,1,0:T(8,128)S(1)}, f32[176,128]{1,0:T(8,128)S(1)}) custom-call(f32[12,128,256]{2,1,0:T(8,128)S(1)} %bitcast.4, f32[3,128,256]{2,1,0:T(8,128)S(1)} %copy-done.2, s32[128,256]{1,0:T(8,128)S(1)} %copy-done.3, f32[16,16,256]{2,1,0:T(8,128)S(1)} %collective-permute-done.ra, ...), custom_call_target="tpu_custom_call" | custom-call | tf_op jit(solution)/shard_map/extend/pallas_call | solution.py:172
  23.1 1.5 %collective-permute-start.2 = (f32[2,160,128]{2,1,0:T(8,128)S(1)}, f32[2,160,128]{2,1,0:T(8,128)S(1)}, u32[]{:S(2)}, u32[]{:S(2)}) collective-permute-start(f32[2,160,128]{2,1,0:T(8,128)S(1)} %get-tuple-element.15), channel_id=1, source_target_pairs={{0,4},{4,8},{8,12},{12,16},{16,20},{20,24},{24,28},{28,32},{32,36}... | collective-permute-start | bytes 491528 | tf_op jit(solution)/shard_map/ppermute | solution.py:378
  24.6 5.7 %collective-permute-start.3 = (f32[2,160,128]{2,1,0:T(8,128)S(1)}, f32[2,160,128]{2,1,0:T(8,128)S(1)}, u32[]{:S(2)}, u32[]{:S(2)}) collective-permute-start(f32[2,160,128]{2,1,0:T(8,128)S(1)} %get-tuple-element.16), channel_id=1, source_target_pairs={{4,0},{8,4},{12,8},{16,12},{20,16},{24,20},{28,24},{32,28},{36,32}... | collective-permute-start | bytes 491528 | tf_op jit(solution)/shard_map/ppermute | solution.py:379
  30.3 0.0 copy-start
  30.3 2.2 %copy-done = f32[3,16,176,128]{3,2,1,0:T(8,128)S(1)} copy-done((f32[3,16,176,128]{3,2,1,0:T(8,128)S(1)}, f32[3,16,176,128]{3,2,1,0:T(8,128)}, u32[]{:S(2)}) %copy-start) | copy-done | bytes 4325400
  32.5 54.0 %interior.1.inner = f32[2,12,144,128]{3,2,1,0:T(8,128)S(1)} custom-call(f32[3,16,176,128]{3,2,1,0:T(8,128)S(1)} %copy-done, f32[176,128]{1,0:T(8,128)S(1)} %get-tuple-element.14.cor), custom_call_target="tpu_custom_call" | custom-call | flops 129761280 | bytes 4325376 | tf_op jit(solution)/shard_map/interior/pallas_call | solution.py:291
  86.5 0.0 collective-permute-done.2.got_low
  86.5 0.0 collective-permute-done.3.got_high
  86.5 33.2 %edges.1 = f32[12,128,256]{2,1,0:T(8,128)} custom-call(f32[3,16,176,128]{3,2,1,0:T(8,128)} %get-tuple-element.13.tiles, f32[176,128]{1,0:T(8,128)S(1)} %get-tuple-element.14.cor, f32[2,160,128]{2,1,0:T(8,128)S(1)} %collective-permute-done.2.got_low, f32[2,160,128]{2,1,0:T(8,128)S(1)} %collective-permute-done.3.got_high, f32[2,12,144,128]{3,2,1,0:T(8,128)S(1)} %interior.1.inner), custom_call_target="tpu_custom_call" | custom-call | tf_op jit(solution)/shard_map/edges/pallas_call | solution.py:339
Async XLA Ops:
  0.0 1.4 %copy-start.1 = (f32[4,3,128,256]{3,2,1,0:T(8,128)S(1)}, f32[4,3,128,256]{3,2,1,0:T(8,128)}, u32[]{:S(2)}) copy-start(f32[4,3,128,256]{3,2,1,0:T(8,128)} %param.3) | copy-start | bytes 4718596
  1.4 1.0 copy-start.2
  2.4 0.9 copy-start.3
  3.4 13.5 %collective-permute-start = (f32[16,16,256]{2,1,0:T(8,128)S(1)}, f32[16,16,256]{2,1,0:T(8,128)S(1)}, u32[]{:S(2)}, u32[]{:S(2)}) collective-permute-start(f32[16,16,256]{2,1,0:T(8,128)S(1)} %get-tuple-element.11), channel_id=1, source_target_pairs={{1,2},{2,1},{3,127},{5,6},{6,5},{7,123},{9,10},{10,9},{11,119},{13... | collective-permute-start | bytes 786440 | tf_op jit(solution)/shard_map/ppermute | solution.py:375
  13.0 3.9 %collective-permute-start.1 = (f32[16,16,256]{2,1,0:T(8,128)S(1)}, f32[16,16,256]{2,1,0:T(8,128)S(1)}, u32[]{:S(2)}, u32[]{:S(2)}) collective-permute-start(f32[16,16,256]{2,1,0:T(8,128)S(1)} %get-tuple-element.12), channel_id=1, source_target_pairs={{0,1},{1,0},{2,3},{3,2},{4,5},{5,4},{6,7},{7,6},{8,9},{9,8},{10,11... | collective-permute-start | bytes 786440 | tf_op jit(solution)/shard_map/ppermute | solution.py:376
  23.1 63.5 %collective-permute-start.2 = (f32[2,160,128]{2,1,0:T(8,128)S(1)}, f32[2,160,128]{2,1,0:T(8,128)S(1)}, u32[]{:S(2)}, u32[]{:S(2)}) collective-permute-start(f32[2,160,128]{2,1,0:T(8,128)S(1)} %get-tuple-element.15), channel_id=1, source_target_pairs={{0,4},{4,8},{8,12},{12,16},{16,20},{20,24},{24,28},{28,32},{32,36}... | collective-permute-start | bytes 491528 | tf_op jit(solution)/shard_map/ppermute | solution.py:378
  24.6 62.0 %collective-permute-start.3 = (f32[2,160,128]{2,1,0:T(8,128)S(1)}, f32[2,160,128]{2,1,0:T(8,128)S(1)}, u32[]{:S(2)}, u32[]{:S(2)}) collective-permute-start(f32[2,160,128]{2,1,0:T(8,128)S(1)} %get-tuple-element.16), channel_id=1, source_target_pairs={{4,0},{8,4},{12,8},{16,12},{20,16},{24,20},{28,24},{32,28},{36,32}... | collective-permute-start | bytes 491528 | tf_op jit(solution)/shard_map/ppermute | solution.py:379
  30.3 2.2 %copy-start = (f32[3,16,176,128]{3,2,1,0:T(8,128)S(1)}, f32[3,16,176,128]{3,2,1,0:T(8,128)}, u32[]{:S(2)}) copy-start(f32[3,16,176,128]{3,2,1,0:T(8,128)} %get-tuple-element.13.tiles) | copy-start | bytes 12976132
where the time goes:
time: 120 us
  Pallas kernels  93.5 us (78%)
  starting transfers between devices  16.9 us (14%)
  local copies, waits for them, and re-layouts  5.53 us (5%)
  waiting for transfers between devices  3.77 us (3%)
    pallas_call x1, Pallas kernels, interior(): pl.pallas_call(interior_kernel, in_specs=[pl.BlockSpec((2,) + tiles.shape...  54 us
    pallas_call x1, Pallas kernels, edges(): pl.pallas_call(edge_kernel, grid=(1,), in_specs=[pl.BlockSpec((1,) + tile...  33.2 us
    ppermute x1, starting transfers between devices, body(): ra = lax.ppermute(to_a, axes, pairs_a)  9.59 us
    pallas_call x1, Pallas kernels, extend(): pl.pallas_call(extend_kernel, in_specs=[vmem] * 5, out_specs=[vmem] * 4,...  6.22 us
    ppermute x1, starting transfers between devices, body(): got_high = lax.ppermute(send_low, 'lon', west)  5.68 us
    unnamed x8, local copies, waits for them, and re-layouts  5.53 us
    ppermute x1, waiting for transfers between devices, body(): ra = lax.ppermute(to_a, axes, pairs_a)  3.76 us
  transfers between devices with their start and end apart: 4, of which 1 were waited for; matrix products, arithmetic and copies ran while one was open for 0% of the time, Pallas kernels for 45%

commit v1 on v0

--- a/solution.py
+++ b/solution.py
@@ -117,9 +117,8 @@
         for p, lo, hi in zip(planes, low, high):
             here = pl.ds(at, rows)
             tiles[0, p, here] = lo
-            tiles[1, p, here] = jnp.where(lane < 32, shifted(lo, -96), shifted(hi, 32))
-            edge = jnp.where(lane < 48, shifted(lo, 16), shifted(hi, -16))
-            tiles[2, p, here] = edge
+            tiles[1, p, here] = jnp.where(lane < 96, hi, lo)
+            tiles[2, p, here] = jnp.where(lane < 64, shifted(lo, 32), hi)
             packs.append((lo, hi))
         return packs
 
@@ -185,13 +184,44 @@
     )(x, mixing, land, ra, rb)
 
 
-def substep(src, dst, coef, cor, start, dst_start, span, unroll=1):
+def line_weights():
+    shape = (2 * LANES, LANES)
+    here = lax.rem(lax.broadcasted_iota(jnp.int32, shape, 0), LANES)
+    lane = lax.broadcasted_iota(jnp.int32, shape, 1)
+    gap = lax.rem(here - lane + LANES, LANES)
+
+    def stencil(terms):
+        out = jnp.zeros(shape, jnp.float32)
+        for offset, value in terms:
+            out = jnp.where(gap == offset % LANES, value, out)
+        return out
+
+    east = stencil(((0, 7.0), (1, 7.0), (-1, -1.0), (2, -1.0)))
+    west = stencil(((-1, 7.0), (0, 7.0), (-2, -1.0), (1, -1.0)))
+    lap = stencil(((0, -4.0), (1, 1.0), (-1, 1.0)))
+    diff = stencil(((1, 1.0), (-1, -1.0)))
+    return jnp.concatenate([east, west, lap, diff], axis=1).astype(jnp.bfloat16)
+
+
+def products(src, weights, prod, first, count):
+    for f in range(4):
+        planes = pl.ds(f * K, K)
+        rows = pl.ds(first, count)
+        q = src[planes, rows, :].reshape(K * count, LANES)
+        high = q.astype(jnp.bfloat16)
+        low = (q - high.astype(jnp.float32)).astype(jnp.bfloat16)
+        both = jnp.concatenate([high, low], axis=1)
+        got = jnp.dot(both, weights[...], preferred_element_type=jnp.float32)
+        for j in range(4 if f < 3 else 3):
+            prod[j, planes, rows, :] = got[:, j * LANES : (j + 1) * LANES].reshape(K, count, LANES)
+
+
+def substep(src, dst, coef, cor, prod, mask, start, dst_start, span, unroll=2):
     def load(ref, p, t):
         return ref[p, pl.ds(start + t, 8, stride=span), :]
 
-    def face(prev, here, nxt, nxt2):
-        a = here + nxt
-        return a, 7.0 * a - (prev + nxt2)
+    def line(j, p, t):
+        return prod[j, p, pl.ds(start + t, 8, stride=span), :]
 
     def density(t, k):
         return -0.25 * THERMAL * load(src, k, t) + 0.25 * HALINE * load(src, K + k, t)
@@ -205,11 +235,11 @@
     def fluxes(t):
         out = [None] * STATE
         for k in range(K):
-            order = [3, 0, 1, 2]
             speed = None
-            for f in order:
+            for f in (3, 0, 1, 2):
                 p = f * K + k
-                a, value = face(load(src, p, t - 1), load(src, p, t), load(src, p, t + 1), load(src, p, t + 2))
+                a = load(src, p, t) + load(src, p, t + 1)
+                value = 7.0 * a - (load(src, p, t - 1) + load(src, p, t + 2))
                 if f == 3:
                     speed = a
                 out[p] = speed * value
@@ -217,41 +247,37 @@
 
     def row(t, carry):
         below_flux, p_prev, p_here = carry
-        wet = coef(15)(t)
+        wet = coef(STATE + K, t) * mask
         wet24 = wet * (1.0 / 24.0)
         wet_cor = wet * cor[pl.ds(start + t, 8, stride=span), :]
         p_next = pressures(t + 1)
         above = fluxes(t)
+        grad_lon = None
         for k in range(K):
-            wet_mix = wet * coef(STATE + k)(t)
-            speed = None
-            for f in (2, 3, 0, 1):
+            wet_mix = wet * coef(STATE + k, t)
+            drop = -0.25 * THERMAL * line(3, k, t) + 0.25 * HALINE * line(3, K + k, t)
+            grad_lon = drop if k == 0 else grad_lon + drop
+            u = load(src, 2 * K + k, t)
+            mean = 3.0 * u + 0.5 * line(2, 2 * K + k, t)
+            half = 0.5 * line(3, 2 * K + k, t)
+            east_speed, west_speed = mean + half, mean - half
+            for f in range(4):
                 p = f * K + k
                 q = load(src, p, t)
-                east = shifted(q, -1)
-                west = shifted(q, 1)
-                a, value = face(west, q, east, shifted(q, -2))
-                if f == 2:
-                    speed = a
-                flux = speed * value
-                adv = (flux - shifted(flux, 1)) + (above[p] - below_flux[p])
-                lap = (east + west) + (load(src, p, t + 1) + load(src, p, t - 1))
+                adv = (east_speed * line(0, p, t) - west_speed * line(1, p, t)) + (above[p] - below_flux[p])
+                lap = line(2, p, t) + (load(src, p, t + 1) + load(src, p, t - 1))
                 if f < 2:
                     if 0 < k < K - 1:
-                        lap = lap + 0.5 * (load(src, p - 1, t) + load(src, p + 1, t)) - 5.0 * q
+                        lap = lap + (0.5 * (load(src, p - 1, t) + load(src, p + 1, t)) - q)
                     elif k == 0:
-                        lap = lap + 0.5 * load(src, p + 1, t) - 4.5 * q
+                        lap = lap + 0.5 * (load(src, p + 1, t) - q)
                     else:
-                        lap = lap + 0.5 * load(src, p - 1, t) - 4.5 * q
-                else:
-                    lap = lap - 4.0 * q
+                        lap = lap + 0.5 * (load(src, p - 1, t) - q)
                 new = q + (wet_mix * lap - wet24 * adv)
                 if f == 2:
-                    grad = shifted(p_here[k], -1) - shifted(p_here[k], 1)
-                    new = new + (wet_cor * load(src, p + K, t) - wet * grad)
+                    new = new + (wet_cor * load(src, p + K, t) - wet * grad_lon)
                 if f == 3:
-                    grad = p_next[k] - p_prev[k]
-                    new = new - (wet_cor * load(src, p - K, t) + wet * grad)
+                    new = new - (wet_cor * load(src, p - K, t) + wet * (p_next[k] - p_prev[k]))
                 dst[p, pl.ds(dst_start + t, 8, stride=span), :] = new
         return above, p_here, p_next
 
@@ -259,8 +285,13 @@
     lax.fori_loop(0, span, row, init, unroll=unroll)
 
 
-def window(tile, cor, even, odd, out):
+def window(tile, cor, seams, weights, prod, even, odd, out):
     span_rows = tile.shape[1] - 2 * PAD
+    lane = lax.broadcasted_iota(jnp.int32, (8, LANES), 1)
+    room = jnp.full((8, LANES), LANES, jnp.int32)
+    for seam in seams:
+        after = lax.rem(lane - seam + LANES, LANES)
+        room = jnp.minimum(room, jnp.minimum(after, LANES - 1 - after))
     src = tile
     for s in range(STEPS):
         span = SPANS[s]
@@ -269,18 +300,24 @@
         start = PAD + 2 * (s + 1) - spare
         dst = out if s == STEPS - 1 else (even if s % 2 == 0 else odd)
         dst_start = PAD - spare if s == STEPS - 1 else start
-
-        def coef(p, start=start, span=span):
-            return lambda t: tile[p, pl.ds(start + t, 8, stride=span), :]
-
-        substep(src, dst, coef, cor, start, dst_start, span)
+        first = start // 16 * 16
+        count = -(-(start + 8 * span) // 16) * 16 - first
+        products(src, weights, prod, first, count)
+
+        def coef(p, t, start=start, span=span):
+            return tile[p, pl.ds(start + t, 8, stride=span), :]
+
+        mask = jnp.where(room >= 2 * (s + 1), 1.0, 0.0)
+        substep(src, dst, coef, cor, prod, mask, start, dst_start, span)
         src = dst
 
 
-def interior_kernel(tiles, cor, out, even, odd):
+def interior_kernel(tiles, cor, out, even, odd, weights, prod):
+    weights[...] = line_weights()
+
     @pl.loop(0, 2)
     def _(i):
-        window(tiles.at[i], cor, even, odd, out.at[i])
+        window(tiles.at[i], cor, (96 * i,), weights, prod, even, odd, out.at[i])
 
 
 def interior(tiles, cor):
@@ -294,28 +331,34 @@
         out_specs=pl.BlockSpec((2, STATE, block + 2 * PAD, LANES), lambda g: (0, 0, 0, 0)),
         grid=(1,),
         out_shape=jax.ShapeDtypeStruct((2, STATE, block + 2 * PAD, LANES), jnp.float32),
-        scratch_shapes=[pltpu.VMEM((STATE, rows, LANES), jnp.float32)] * 2,
+        scratch_shapes=[
+            pltpu.VMEM((STATE, rows, LANES), jnp.float32),
+            pltpu.VMEM((STATE, rows, LANES), jnp.float32),
+            pltpu.VMEM((2 * LANES, 4 * LANES), jnp.bfloat16),
+            pltpu.VMEM((4, STATE, rows, LANES), jnp.float32),
+        ],
         compiler_params=params(),
         cost_estimate=pl.CostEstimate(flops=STEPS * 30 * cells, transcendentals=0, bytes_accessed=8 * cells),
         name="interior",
     )(tiles, cor)
 
 
-def edge_kernel(tiles, cor, got_low, got_high, inner, out, tile, even, odd, edge):
+def edge_kernel(tiles, cor, got_low, got_high, inner, out, tile, even, odd, edge, weights, prod):
     span = got_low.shape[1]
     block = out.shape[1]
+    weights[...] = line_weights()
 
     @pl.loop(0, span // 8)
     def _(g):
         r = pl.multiple_of(g * 8, 8)
         lane = lax.broadcasted_iota(jnp.int32, (8, LANES), 1)
         for p in range(PLANES):
-            left = shifted(got_low[p // 8, pl.ds(r, 8)], -16 * (p % 8))
-            right = shifted(got_high[p // 8, pl.ds(r, 8)], 112 - 16 * (p % 8))
+            left = shifted(got_low[p // 8, pl.ds(r, 8)], 16 - 16 * (p % 8))
+            right = shifted(got_high[p // 8, pl.ds(r, 8)], -16 * (p % 8))
             mid = tiles[0, p, pl.ds(PAD + r, 8)]
-            tile[p, pl.ds(PAD + r, 8)] = jnp.where(lane < 16, left, jnp.where(lane >= 112, right, mid))
-
-    window(tile, cor, even, odd, edge)
+            tile[p, pl.ds(PAD + r, 8)] = jnp.where(lane < 16, right, jnp.where(lane < 32, left, mid))
+
+    window(tile, cor, (16, 64), weights, prod, even, odd, edge)
 
     @pl.loop(0, block // 8)
     def _(g):
@@ -326,8 +369,8 @@
             e = edge[p, here]
             lo = inner[0, p, here]
             hi = inner[1, p, here]
-            out[p, pl.ds(r, 8), :LANES] = jnp.where(lane < 16, shifted(e, -16), jnp.where(lane < 112, lo, shifted(hi, 96)))
-            out[p, pl.ds(r, 8), LANES:] = jnp.where(lane < 80, shifted(hi, -32), shifted(e, 16))
+            out[p, pl.ds(r, 8), :LANES] = jnp.where(lane < 16, shifted(e, -32), jnp.where(lane < 112, lo, hi))
+            out[p, pl.ds(r, 8), LANES:] = jnp.where(lane < 80, hi, e)
 
 
 def edges(tiles, cor, got_low, got_high, inner, cols):
@@ -347,6 +390,8 @@
             pltpu.VMEM((STATE, rows, LANES), f32),
             pltpu.VMEM((STATE, rows, LANES), f32),
             pltpu.VMEM((STATE, block + 2 * PAD, LANES), f32),
+            pltpu.VMEM((2 * LANES, 4 * LANES), jnp.bfloat16),
+            pltpu.VMEM((4, STATE, rows, LANES), f32),
         ],
         compiler_params=params(),
         name="edges",

time: 120 us -> 73.2 us (0.61)
  Pallas kernels: 93.5 us -> 46.8 us
    pallas_call x1, Pallas kernels: 54 us -> 23.6 us  [interior(): pl.pallas_call(interior_kernel, in_specs=[pl.BlockSpec((2,) + tiles.shape...]
    pallas_call x1, Pallas kernels: 33.2 us -> 17.7 us  [edges(): pl.pallas_call(edge_kernel, grid=(1,), in_specs=[pl.BlockSpec((1,) + tile...]
  transfers between devices with their start and end apart: 4 -> 4, of which waited for: 1 -> 1; matrix products, arithmetic and copies ran while one was open for 0% -> 0% of each run, Pallas kernels for 45% -> 32%
where the time goes in v1:
time: 73.2 us; the launch traced here: 73 us
  Pallas kernels  46.8 us (64%)
  starting transfers between devices  16.9 us (23%)
  local copies, waits for them, and re-layouts  5.53 us (8%)
  waiting for transfers between devices  3.77 us (5%)
    pallas_call x1, Pallas kernels, interior(): pl.pallas_call(interior_kernel, in_specs=[pl.BlockSpec((2,) + tiles.shape...  23.6 us
    pallas_call x1, Pallas kernels, edges(): pl.pallas_call(edge_kernel, grid=(1,), in_specs=[pl.BlockSpec((1,) + tile...  17.7 us
    ppermute x1, starting transfers between devices, body(): ra = lax.ppermute(to_a, axes, pairs_a)  9.59 us
    ppermute x1, starting transfers between devices, body(): got_high = lax.ppermute(send_low, 'lon', west)  5.68 us
    unnamed x8, local copies, waits for them, and re-layouts  5.53 us
    pallas_call x1, Pallas kernels, extend(): pl.pallas_call(extend_kernel, in_specs=[vmem] * 5, out_specs=[vmem] * 4,...  5.38 us
    ppermute x1, waiting for transfers between devices, body(): ra = lax.ppermute(to_a, axes, pairs_a)  3.76 us
    ppermute x1, starting transfers between devices, body(): got_low = lax.ppermute(send_high, 'lon', east)  1.51 us
  transfers between devices with their start and end apart: 4, of which 1 were waited for; matrix products, arithmetic and copies ran while one was open for 0% of the time, Pallas kernels for 32%

profile of v1, /device:TPU:9, one launch (start us, length us, event | category | flops | bytes accessed | tf_op | source)
XLA Modules:
  0.0 73.0 jit_solution(5576401273451125050)
XLA Ops:
  0.0 0.0 copy-start.1
  0.0 1.4 %copy-done.1 = f32[4,3,128,256]{3,2,1,0:T(8,128)S(1)} copy-done((f32[4,3,128,256]{3,2,1,0:T(8,128)S(1)}, f32[4,3,128,256]{3,2,1,0:T(8,128)}, u32[]{:S(2)}) %copy-start.1) | copy-done | bytes 1572888
  1.4 0.0 copy-start.2
  1.4 1.0 %copy-done.2 = f32[3,128,256]{2,1,0:T(8,128)S(1)} copy-done((f32[3,128,256]{2,1,0:T(8,128)S(1)}, f32[3,128,256]{2,1,0:T(8,128)}, u32[]{:S(2)}) %copy-start.2) | copy-done | bytes 393240
  2.4 0.0 copy-start.3
  2.4 0.9 %copy-done.3 = s32[128,256]{1,0:T(8,128)S(1)} copy-done((s32[128,256]{1,0:T(8,128)S(1)}, s32[128,256]{1,0:T(8,128)}, u32[]{:S(2)}) %copy-start.3) | copy-done | bytes 131096
  3.3 0.1 pack_rows.1
  3.4 9.6 %collective-permute-start = (f32[16,16,256]{2,1,0:T(8,128)S(1)}, f32[16,16,256]{2,1,0:T(8,128)S(1)}, u32[]{:S(2)}, u32[]{:S(2)}) collective-permute-start(f32[16,16,256]{2,1,0:T(8,128)S(1)} %get-tuple-element.11), channel_id=1, source_target_pairs={{1,2},{2,1},{3,127},{5,6},{6,5},{7,123},{9,10},{10,9},{11,119},{13... | collective-permute-start | bytes 786440 | tf_op jit(solution)/shard_map/ppermute | solution.py:420
  13.0 0.1 collective-permute-start.1
  13.1 3.8 %collective-permute-done.ra = f32[16,16,256]{2,1,0:T(8,128)S(1)} collective-permute-done((f32[16,16,256]{2,1,0:T(8,128)S(1)}, f32[16,16,256]{2,1,0:T(8,128)S(1)}, u32[]{:S(2)}, u32[]{:S(2)}) %collective-permute-start) | collective-permute-done | bytes 262176 | tf_op jit(solution)/shard_map/ppermute | solution.py:420
  16.8 0.0 collective-permute-done.1.rb
  16.8 5.4 %extend.1 = (f32[3,16,176,128]{3,2,1,0:T(8,128)}, f32[2,160,128]{2,1,0:T(8,128)S(1)}, f32[2,160,128]{2,1,0:T(8,128)S(1)}, f32[176,128]{1,0:T(8,128)S(1)}) custom-call(f32[12,128,256]{2,1,0:T(8,128)S(1)} %bitcast.4, f32[3,128,256]{2,1,0:T(8,128)S(1)} %copy-done.2, s32[128,256]{1,0:T(8,128)S(1)} %copy-done.3, f32[16,16,256]{2,1,0:T(8,128)S(1)} %collective-permute-done.ra, ...), custom_call_target="tpu_custom_call" | custom-call | tf_op jit(solution)/shard_map/extend/pallas_call | solution.py:171
  22.2 1.5 %collective-permute-start.2 = (f32[2,160,128]{2,1,0:T(8,128)S(1)}, f32[2,160,128]{2,1,0:T(8,128)S(1)}, u32[]{:S(2)}, u32[]{:S(2)}) collective-permute-start(f32[2,160,128]{2,1,0:T(8,128)S(1)} %get-tuple-element.15), channel_id=1, source_target_pairs={{0,4},{4,8},{8,12},{12,16},{16,20},{20,24},{24,28},{28,32},{32,36}... | collective-permute-start | bytes 491528 | tf_op jit(solution)/shard_map/ppermute | solution.py:423
  23.7 5.7 %collective-permute-start.3 = (f32[2,160,128]{2,1,0:T(8,128)S(1)}, f32[2,160,128]{2,1,0:T(8,128)S(1)}, u32[]{:S(2)}, u32[]{:S(2)}) collective-permute-start(f32[2,160,128]{2,1,0:T(8,128)S(1)} %get-tuple-element.16), channel_id=1, source_target_pairs={{4,0},{8,4},{12,8},{16,12},{20,16},{24,20},{28,24},{32,28},{36,32}... | collective-permute-start | bytes 491528 | tf_op jit(solution)/shard_map/ppermute | solution.py:424
  29.4 0.0 copy-start
  29.4 2.2 %copy-done = f32[3,16,176,128]{3,2,1,0:T(8,128)S(1)} copy-done((f32[3,16,176,128]{3,2,1,0:T(8,128)S(1)}, f32[3,16,176,128]{3,2,1,0:T(8,128)}, u32[]{:S(2)}) %copy-start) | copy-done | bytes 4325400
  31.6 23.6 %interior.1.inner = f32[2,12,144,128]{3,2,1,0:T(8,128)S(1)} custom-call(f32[3,16,176,128]{3,2,1,0:T(8,128)S(1)} %copy-done, f32[176,128]{1,0:T(8,128)S(1)} %get-tuple-element.14.cor), custom_call_target="tpu_custom_call" | custom-call | flops 129761280 | bytes 4325376 | tf_op jit(solution)/shard_map/interior/pallas_call | solution.py:328
  55.3 0.0 collective-permute-done.2.got_low
  55.3 0.0 collective-permute-done.3.got_high
  55.3 17.7 %edges.1 = f32[12,128,256]{2,1,0:T(8,128)} custom-call(f32[3,16,176,128]{3,2,1,0:T(8,128)} %get-tuple-element.13.tiles, f32[176,128]{1,0:T(8,128)S(1)} %get-tuple-element.14.cor, f32[2,160,128]{2,1,0:T(8,128)S(1)} %collective-permute-done.2.got_low, f32[2,160,128]{2,1,0:T(8,128)S(1)} %collective-permute-done.3.got_high, f32[2,12,144,128]{3,2,1,0:T(8,128)S(1)} %interior.1.inner), custom_call_target="tpu_custom_call" | custom-call | tf_op jit(solution)/shard_map/edges/pallas_call | solution.py:382
Async XLA Ops:
  0.0 1.4 %copy-start.1 = (f32[4,3,128,256]{3,2,1,0:T(8,128)S(1)}, f32[4,3,128,256]{3,2,1,0:T(8,128)}, u32[]{:S(2)}) copy-start(f32[4,3,128,256]{3,2,1,0:T(8,128)} %param.3) | copy-start | bytes 4718596
  1.4 1.0 %copy-start.2 = (f32[3,128,256]{2,1,0:T(8,128)S(1)}, f32[3,128,256]{2,1,0:T(8,128)}, u32[]{:S(2)}) copy-start(f32[3,128,256]{2,1,0:T(8,128)} %m.1) | copy-start | bytes 1179652
  2.4 0.9 %copy-start.3 = (s32[128,256]{1,0:T(8,128)S(1)}, s32[128,256]{1,0:T(8,128)}, u32[]{:S(2)}) copy-start(s32[128,256]{1,0:T(8,128)} %w.1) | copy-start | bytes 393220
  3.4 13.5 %collective-permute-start = (f32[16,16,256]{2,1,0:T(8,128)S(1)}, f32[16,16,256]{2,1,0:T(8,128)S(1)}, u32[]{:S(2)}, u32[]{:S(2)}) collective-permute-start(f32[16,16,256]{2,1,0:T(8,128)S(1)} %get-tuple-element.11), channel_id=1, source_target_pairs={{1,2},{2,1},{3,127},{5,6},{6,5},{7,123},{9,10},{10,9},{11,119},{13... | collective-permute-start | bytes 786440 | tf_op jit(solution)/shard_map/ppermute | solution.py:420
  13.0 3.9 %collective-permute-start.1 = (f32[16,16,256]{2,1,0:T(8,128)S(1)}, f32[16,16,256]{2,1,0:T(8,128)S(1)}, u32[]{:S(2)}, u32[]{:S(2)}) collective-permute-start(f32[16,16,256]{2,1,0:T(8,128)S(1)} %get-tuple-element.12), channel_id=1, source_target_pairs={{0,1},{1,0},{2,3},{3,2},{4,5},{5,4},{6,7},{7,6},{8,9},{9,8},{10,11... | collective-permute-start | bytes 786440 | tf_op jit(solution)/shard_map/ppermute | solution.py:421
  22.2 33.1 %collective-permute-start.2 = (f32[2,160,128]{2,1,0:T(8,128)S(1)}, f32[2,160,128]{2,1,0:T(8,128)S(1)}, u32[]{:S(2)}, u32[]{:S(2)}) collective-permute-start(f32[2,160,128]{2,1,0:T(8,128)S(1)} %get-tuple-element.15), channel_id=1, source_target_pairs={{0,4},{4,8},{8,12},{12,16},{16,20},{20,24},{24,28},{28,32},{32,36}... | collective-permute-start | bytes 491528 | tf_op jit(solution)/shard_map/ppermute | solution.py:423
  23.7 31.6 %collective-permute-start.3 = (f32[2,160,128]{2,1,0:T(8,128)S(1)}, f32[2,160,128]{2,1,0:T(8,128)S(1)}, u32[]{:S(2)}, u32[]{:S(2)}) collective-permute-start(f32[2,160,128]{2,1,0:T(8,128)S(1)} %get-tuple-element.16), channel_id=1, source_target_pairs={{4,0},{8,4},{12,8},{16,12},{20,16},{24,20},{28,24},{32,28},{36,32}... | collective-permute-start | bytes 491528 | tf_op jit(solution)/shard_map/ppermute | solution.py:424
  29.4 2.2 %copy-start = (f32[3,16,176,128]{3,2,1,0:T(8,128)S(1)}, f32[3,16,176,128]{3,2,1,0:T(8,128)}, u32[]{:S(2)}) copy-start(f32[3,16,176,128]{3,2,1,0:T(8,128)} %get-tuple-element.13.tiles) | copy-start | bytes 12976132

commit v2 on v1

--- a/solution.py
+++ b/solution.py
@@ -19,7 +19,7 @@
 
 STATE = 4 * K
 PLANES = STATE + K + 1
-VMEM_LIMIT = 48 * 1024 * 1024
+VMEM_LIMIT = 24 * 1024 * 1024
 SPANS = (21, 19, 19, 19, 19, 17, 17, 17)
 
 
@@ -31,42 +31,36 @@
     return pltpu.roll(x, by % LANES, 1)
 
 
-def pack_rows_kernel(xl, xh, ml, mh, wl, wh, to_a, to_b):
+def pack_rows_kernel(x, m, w, to_a, to_b, wet, sems):
     even = lax.rem(lax.axis_index("lat"), 2) == 0
-
-    def fill(dest, x, m, w):
-        dest[:STATE] = x[...]
-        dest[STATE : STATE + K] = m[...]
-        dest[STATE + K] = TIMESTEP * w[...].astype(jnp.float32)
-
-    @pl.when(even)
-    def _():
-        fill(to_b, xh, mh, wh)
-        fill(to_a, xl, ml, wl)
-
-    @pl.when(jnp.logical_not(even))
-    def _():
-        fill(to_b, xl, ml, wl)
-        fill(to_a, xh, mh, wh)
+    last = x.shape[1] - HALO
+    starts = (jnp.where(even, 0, last), jnp.where(even, last, 0))
+    copies = []
+    for i, dest in enumerate((to_a, to_b)):
+        rows = pl.ds(pl.multiple_of(starts[i], HALO), HALO)
+        copies.append(pltpu.make_async_copy(x.at[:, rows, :], dest.at[pl.ds(0, STATE)], sems.at[3 * i]))
+        copies.append(pltpu.make_async_copy(m.at[:, rows, :], dest.at[pl.ds(STATE, K)], sems.at[3 * i + 1]))
+        copies.append(pltpu.make_async_copy(w.at[rows, :], wet.at[i], sems.at[3 * i + 2]))
+    for copy in copies:
+        copy.start()
+    for copy in copies:
+        copy.wait()
+    for i, dest in enumerate((to_a, to_b)):
+        dest[STATE + K] = TIMESTEP * wet[i].astype(jnp.float32)
 
 
 def pack_rows(x, mixing, land):
-    rows, cols = land.shape
-    last = rows // HALO - 1
-    specs = []
-    for lead in ((STATE,), (K,), ()):
-        for at in (0, last):
-            specs.append(pl.BlockSpec(lead + (HALO, cols), functools.partial(lambda at, n, g: (0,) * n + (at, 0), at, len(lead))))
+    cols = land.shape[1]
     slab = jax.ShapeDtypeStruct((PLANES, HALO, cols), jnp.float32)
     return pl.pallas_call(
         pack_rows_kernel,
-        grid=(1,),
-        in_specs=specs,
-        out_specs=[pl.BlockSpec(slab.shape, lambda g: (0, 0, 0))] * 2,
+        in_specs=[pl.BlockSpec(memory_space=pltpu.HBM)] * 3,
+        out_specs=[pl.BlockSpec(memory_space=pltpu.VMEM)] * 2,
         out_shape=[slab, slab],
+        scratch_shapes=[pltpu.VMEM((2, HALO, cols), jnp.int32), pltpu.SemaphoreType.DMA((6,))],
         compiler_params=params(),
         name="pack_rows",
-    )(x, x, mixing, mixing, land, land)
+    )(x, mixing, land)
 
 
 def fold(slab):
@@ -85,66 +79,37 @@
     return dot(dot(left, flat), right).reshape(slab.shape)
 
 
-def extend_kernel(x, m, w, ra, rb, tiles, send_low, send_high, cor, south, north):
+def place(at, source, tiles, send_low, send_high):
+    lane = lax.broadcasted_iota(jnp.int32, (8, LANES), 1)
+    for group in range(PLANES // 8):
+        low = jnp.zeros((8, LANES), jnp.float32)
+        high = jnp.zeros((8, LANES), jnp.float32)
+        for q in range(8):
+            p = group * 8 + q
+            lo, hi = source(p)
+            here = pl.ds(PAD + at, 8)
+            tiles[0][p, here] = lo
+            tiles[1][p, here] = jnp.where(lane < 96, hi, lo)
+            tiles[2][p, here] = jnp.where(lane < 64, shifted(lo, 32), hi)
+            mine = jnp.logical_and(lane >= 16 * q, lane < 16 * q + 16)
+            low = jnp.where(mine, shifted(lo, 16 * q), low)
+            high = jnp.where(mine, shifted(hi, 16 * q - 112), high)
+        send_low[group, pl.ds(at, 8)] = low
+        send_high[group, pl.ds(at, 8)] = high
+
+
+def extend_kernel(x_all, m_all, w_all, tile0, tile1, tile2, send_low, send_high, cor, x, m, w, sems):
+    pairs = ((x_all, x), (m_all, m), (w_all, w))
+    copies = [pltpu.make_async_copy(a, b, sems.at[i]) for i, (a, b) in enumerate(pairs)]
+    for copy in copies:
+        copy.start()
     lat = lax.axis_index("lat")
-    even = lax.rem(lat, 2) == 0
     block = x.shape[1]
     total = block * lax.axis_size("lat")
-
-    @pl.when(even)
-    def _():
-        north[...] = rb[...]
-        south[...] = ra[...]
-
-    @pl.when(jnp.logical_not(even))
-    def _():
-        south[...] = rb[...]
-
-        @pl.when(lat == lax.axis_size("lat") - 1)
-        def _():
-            north[...] = fold(ra[...])
-
-        @pl.when(lat != lax.axis_size("lat") - 1)
-        def _():
-            north[...] = ra[...]
-
     row = lax.broadcasted_iota(jnp.int32, cor.shape, 0) + (lat * block - HALO - PAD)
     cor[...] = jnp.sin(jnp.pi * (row.astype(jnp.float32) + 0.5) / total - jnp.pi / 2)
-
-    def put(at, planes, low, high, rows):
-        lane = lax.broadcasted_iota(jnp.int32, (rows, LANES), 1)
-        packs = []
-        for p, lo, hi in zip(planes, low, high):
-            here = pl.ds(at, rows)
-            tiles[0, p, here] = lo
-            tiles[1, p, here] = jnp.where(lane < 96, hi, lo)
-            tiles[2, p, here] = jnp.where(lane < 64, shifted(lo, 32), hi)
-            packs.append((lo, hi))
-        return packs
-
-    def rows_at(at, source, rows):
-        lane = lax.broadcasted_iota(jnp.int32, (rows, LANES), 1)
-        for group in range(PLANES // 8):
-            low = jnp.zeros((rows, LANES), jnp.float32)
-            high = jnp.zeros((rows, LANES), jnp.float32)
-            for q in range(8):
-                p = group * 8 + q
-                lo, hi = source(p)
-                put(PAD + at, [p], [lo], [hi], rows)
-                mine = jnp.logical_and(lane >= 16 * q, lane < 16 * q + 16)
-                low = jnp.where(mine, shifted(lo, 16 * q), low)
-                high = jnp.where(mine, shifted(hi, 16 * q - 112), high)
-            send_low[group, pl.ds(at, rows)] = low
-            send_high[group, pl.ds(at, rows)] = high
-
-    def from_slab(ref, r):
-        def source(p):
-            return ref[p, pl.ds(r, 8), :LANES], ref[p, pl.ds(r, 8), LANES:]
-        return source
-
-    for r in range(0, HALO, 8):
-        rows_at(r, from_slab(south, r), 8)
-        rows_at(HALO + block + r, from_slab(north, r), 8)
+    for copy in copies:
+        copy.wait()
 
     @pl.loop(0, block // 8)
     def _(g):
@@ -160,28 +125,77 @@
                 TIMESTEP * w[pl.ds(r, 8), LANES:].astype(jnp.float32),
             )
 
-        rows_at(HALO + r, source, 8)
-
-
-def extend(x, mixing, land, ra, rb):
-    block, cols = land.shape
+        place(HALO + r, source, (tile0, tile1, tile2), send_low, send_high)
+
+
+def halo_rows_kernel(ra, rb, t0, t1, t2, sl, sh, tile0, tile1, tile2, send_low, send_high, folded):
+    del t0, t1, t2, sl, sh
+    lat = lax.axis_index("lat")
+    north_at = tile0.shape[1] - 2 * PAD - HALO
+
+    def put(at, slab):
+        for r in range(0, HALO, 8):
+
+            def source(p, r=r):
+                return slab[p, pl.ds(r, 8), :LANES], slab[p, pl.ds(r, 8), LANES:]
+
+            place(at + r, source, (tile0, tile1, tile2), send_low, send_high)
+
+    @pl.when(lax.rem(lat, 2) == 0)
+    def _():
+        put(0, ra)
+        put(north_at, rb)
+
+    @pl.when(lax.rem(lat, 2) == 1)
+    def _():
+        put(0, rb)
+
+        @pl.when(lat == lax.axis_size("lat") - 1)
+        def _():
+            folded[...] = fold(ra[...])
+
+        @pl.when(lat != lax.axis_size("lat") - 1)
+        def _():
+            folded[...] = ra[...]
+
+        put(north_at, folded)
+
+
+def extend(x, mixing, land):
+    block = land.shape[0]
     span = block + 2 * HALO
     f32 = jnp.float32
     vmem = pl.BlockSpec(memory_space=pltpu.VMEM)
+    tile = jax.ShapeDtypeStruct((PLANES, span + 2 * PAD, LANES), f32)
+    send = jax.ShapeDtypeStruct((PLANES // 8, span, LANES), f32)
     return pl.pallas_call(
         extend_kernel,
-        in_specs=[vmem] * 5,
-        out_specs=[vmem] * 4,
-        out_shape=[
-            jax.ShapeDtypeStruct((3, PLANES, span + 2 * PAD, LANES), f32),
-            jax.ShapeDtypeStruct((PLANES // 8, span, LANES), f32),
-            jax.ShapeDtypeStruct((PLANES // 8, span, LANES), f32),
-            jax.ShapeDtypeStruct((span + 2 * PAD, LANES), f32),
+        in_specs=[pl.BlockSpec(memory_space=pltpu.HBM)] * 3,
+        out_specs=[vmem] * 6,
+        out_shape=[tile, tile, tile, send, send, jax.ShapeDtypeStruct((span + 2 * PAD, LANES), f32)],
+        scratch_shapes=[
+            pltpu.VMEM(x.shape, f32),
+            pltpu.VMEM(mixing.shape, f32),
+            pltpu.VMEM(land.shape, jnp.int32),
+            pltpu.SemaphoreType.DMA((3,)),
         ],
-        scratch_shapes=[pltpu.VMEM((PLANES, HALO, cols), f32)] * 2,
         compiler_params=params(),
         name="extend",
-    )(x, mixing, land, ra, rb)
+    )(x, mixing, land)
+
+
+def halo_rows(ra, rb, *parts):
+    vmem = pl.BlockSpec(memory_space=pltpu.VMEM)
+    return pl.pallas_call(
+        halo_rows_kernel,
+        in_specs=[vmem] * 7,
+        out_specs=[vmem] * 5,
+        out_shape=[jax.ShapeDtypeStruct(part.shape, part.dtype) for part in parts],
+        input_output_aliases={i + 2: i for i in range(5)},
+        scratch_shapes=[pltpu.VMEM(ra.shape, jnp.float32)],
+        compiler_params=params(),
+        name="halo_rows",
+    )(ra, rb, *parts)
 
 
 def line_weights():
@@ -312,38 +326,33 @@
         src = dst
 
 
-def interior_kernel(tiles, cor, out, even, odd, weights, prod):
+def interior_kernel(seam, tile, cor, out, even, odd, weights, prod):
     weights[...] = line_weights()
-
-    @pl.loop(0, 2)
-    def _(i):
-        window(tiles.at[i], cor, (96 * i,), weights, prod, even, odd, out.at[i])
-
-
-def interior(tiles, cor):
-    rows = tiles.shape[2]
+    window(tile, cor, (seam,), weights, prod, even, odd, out)
+
+
+def interior(tile, cor, seam):
+    rows = tile.shape[1]
     block = rows - 2 * PAD - 2 * HALO
     vmem = pl.BlockSpec(memory_space=pltpu.VMEM)
-    cells = 2 * STATE * rows * LANES
+    f32 = jnp.float32
     return pl.pallas_call(
-        interior_kernel,
-        in_specs=[pl.BlockSpec((2,) + tiles.shape[1:], lambda g: (0, 0, 0, 0)), pl.BlockSpec(cor.shape, lambda g: (0, 0))],
-        out_specs=pl.BlockSpec((2, STATE, block + 2 * PAD, LANES), lambda g: (0, 0, 0, 0)),
-        grid=(1,),
-        out_shape=jax.ShapeDtypeStruct((2, STATE, block + 2 * PAD, LANES), jnp.float32),
+        functools.partial(interior_kernel, seam),
+        in_specs=[vmem, vmem],
+        out_specs=vmem,
+        out_shape=jax.ShapeDtypeStruct((STATE, block + 2 * PAD, LANES), f32),
         scratch_shapes=[
-            pltpu.VMEM((STATE, rows, LANES), jnp.float32),
-            pltpu.VMEM((STATE, rows, LANES), jnp.float32),
+            pltpu.VMEM((STATE, rows, LANES), f32),
+            pltpu.VMEM((STATE, rows, LANES), f32),
             pltpu.VMEM((2 * LANES, 4 * LANES), jnp.bfloat16),
-            pltpu.VMEM((4, STATE, rows, LANES), jnp.float32),
+            pltpu.VMEM((4, STATE, rows, LANES), f32),
         ],
         compiler_params=params(),
-        cost_estimate=pl.CostEstimate(flops=STEPS * 30 * cells, transcendentals=0, bytes_accessed=8 * cells),
         name="interior",
-    )(tiles, cor)
-
-
-def edge_kernel(tiles, cor, got_low, got_high, inner, out, tile, even, odd, edge, weights, prod):
+    )(tile, cor)
+
+
+def edge_kernel(start, cor, got_low, got_high, inner0, inner1, out, tile, even, odd, edge, weights, prod):
     span = got_low.shape[1]
     block = out.shape[1]
     weights[...] = line_weights()
@@ -355,7 +364,7 @@
         for p in range(PLANES):
             left = shifted(got_low[p // 8, pl.ds(r, 8)], 16 - 16 * (p % 8))
             right = shifted(got_high[p // 8, pl.ds(r, 8)], -16 * (p % 8))
-            mid = tiles[0, p, pl.ds(PAD + r, 8)]
+            mid = start[p, pl.ds(PAD + r, 8)]
             tile[p, pl.ds(PAD + r, 8)] = jnp.where(lane < 16, right, jnp.where(lane < 32, left, mid))
 
     window(tile, cor, (16, 64), weights, prod, even, odd, edge)
@@ -367,24 +376,22 @@
         for p in range(STATE):
             here = pl.ds(PAD + r, 8)
             e = edge[p, here]
-            lo = inner[0, p, here]
-            hi = inner[1, p, here]
+            lo = inner0[p, here]
+            hi = inner1[p, here]
             out[p, pl.ds(r, 8), :LANES] = jnp.where(lane < 16, shifted(e, -32), jnp.where(lane < 112, lo, hi))
             out[p, pl.ds(r, 8), LANES:] = jnp.where(lane < 80, hi, e)
 
 
-def edges(tiles, cor, got_low, got_high, inner, cols):
-    rows = tiles.shape[2]
+def edges(start, cor, got_low, got_high, inner0, inner1):
+    rows = start.shape[1]
     block = rows - 2 * PAD - 2 * HALO
-    whole = lambda a: pl.BlockSpec(a.shape, functools.partial(lambda n, g: (0,) * n, len(a.shape)))
     f32 = jnp.float32
-    shape = jax.ShapeDtypeStruct((STATE, block, cols), f32)
+    vmem = pl.BlockSpec(memory_space=pltpu.VMEM)
     return pl.pallas_call(
         edge_kernel,
-        grid=(1,),
-        in_specs=[pl.BlockSpec((1,) + tiles.shape[1:], lambda g: (2, 0, 0, 0)), whole(cor), whole(got_low), whole(got_high), whole(inner)],
-        out_specs=whole(shape),
-        out_shape=shape,
+        in_specs=[vmem] * 6,
+        out_specs=vmem,
+        out_shape=jax.ShapeDtypeStruct((STATE, block, 2 * LANES), f32),
         scratch_shapes=[
             pltpu.VMEM((PLANES, rows, LANES), f32),
             pltpu.VMEM((STATE, rows, LANES), f32),
@@ -395,7 +402,7 @@
         ],
         compiler_params=params(),
         name="edges",
-    )(tiles, cor, got_low, got_high, inner)
+    )(start, cor, got_low, got_high, inner0, inner1)
 
 
 def body(ocean_state, mixing, land_sea):
@@ -419,11 +426,14 @@
     to_a, to_b = pack_rows(x, mixing, land_sea)
     ra = lax.ppermute(to_a, axes, pairs_a)
     rb = lax.ppermute(to_b, axes, pairs_b)
-    tiles, send_low, send_high, cor = extend(x, mixing, land_sea, ra, rb)
+    *parts, cor = extend(x, mixing, land_sea)
+    tile0, tile1, tile2, send_low, send_high = halo_rows(ra, rb, *parts)
+    inner0 = interior(tile0, cor, 0)
+    send_low, send_high, inner0 = lax.optimization_barrier((send_low, send_high, inner0))
     got_low = lax.ppermute(send_high, "lon", east)
     got_high = lax.ppermute(send_low, "lon", west)
-    inner = interior(tiles, cor)
-    out = edges(tiles, cor, got_low, got_high, inner, cols)
+    inner1 = interior(tile1, cor, 96)
+    out = edges(tile2, cor, got_low, got_high, inner0, inner1)
     return out.reshape(ocean_state.shape)
 
 

time: 73.2 us -> 66.6 us (0.910)
  waiting for transfers between devices: 3.77 us -> 1.06 us
  local copies, waits for them, and re-layouts: 5.53 us -> 3.31 us
  Pallas kernels: 46.8 us -> 44.9 us
    ppermute x1, waiting for transfers between devices: 3.76 us -> 1.06 us  [body(): ra = lax.ppermute(to_a, axes, pairs_a)]
    unnamed x8 -> x6, local copies, waits for them, and re-layouts: 5.53 us -> 3.31 us
    pallas_call x4 -> x6, Pallas kernels: 46.8 us -> 44.9 us  [the longest x2 24.3 us: interior(): pl.pallas_call(functools.partial(interior_kernel, seam), in_specs=[vmem,...]
  transfers between devices with their start and end apart: 4 -> 4, of which waited for: 1 -> 1; matrix products, arithmetic and copies ran while one was open for 0% -> 0% of each run, Pallas kernels for 32% -> 22%
where the time goes in v2:
time: 66.6 us; the launch traced here: 66.4 us
  Pallas kernels  44.9 us (67%)
  starting transfers between devices  17.1 us (26%)
  local copies, waits for them, and re-layouts  3.31 us (5%)
  waiting for transfers between devices  1.06 us (2%)
    pallas_call x2, Pallas kernels, interior(): pl.pallas_call(functools.partial(interior_kernel, seam), in_specs=[vmem,...  24.3 us
    pallas_call x1, Pallas kernels, edges(): pl.pallas_call(edge_kernel, in_specs=[vmem] * 6, out_specs=vmem, out_shap...  16.3 us
    ppermute x1, starting transfers between devices, body(): ra = lax.ppermute(to_a, axes, pairs_a)  9.59 us
    ppermute x1, starting transfers between devices, body(): got_high = lax.ppermute(send_low, 'lon', west)  5.82 us
    unnamed x6, local copies, waits for them, and re-layouts  3.31 us
    pallas_call x1, Pallas kernels, extend(): pl.pallas_call(extend_kernel, in_specs=[pl.BlockSpec(memory_space=pltpu.H...  2.7 us
    ppermute x1, starting transfers between devices, body(): got_low = lax.ppermute(send_high, 'lon', east)  1.57 us
    pallas_call x1, Pallas kernels, halo_rows(): pl.pallas_call(halo_rows_kernel, in_specs=[vmem] * 7, out_specs=[vmem] *...  1.38 us
  transfers between devices with their start and end apart: 4, of which 1 were waited for; matrix products, arithmetic and copies ran while one was open for 0% of the time, Pallas kernels for 22%

profile of v2, /device:TPU:9, one launch (start us, length us, event | category | flops | bytes accessed | tf_op | source)
XLA Modules:
  0.0 66.4 jit_solution(5517572553122535266)
XLA Ops:
  0.0 0.0 copy-start
  0.0 1.4 %copy-done = f32[4,3,128,256]{3,2,1,0:T(8,128)S(1)} copy-done((f32[4,3,128,256]{3,2,1,0:T(8,128)S(1)}, f32[4,3,128,256]{3,2,1,0:T(8,128)}, u32[]{:S(2)}) %copy-start) | copy-done | bytes 1572888
  1.4 0.0 copy-start.1
  1.4 1.0 %copy-done.1 = f32[3,128,256]{2,1,0:T(8,128)S(1)} copy-done((f32[3,128,256]{2,1,0:T(8,128)S(1)}, f32[3,128,256]{2,1,0:T(8,128)}, u32[]{:S(2)}) %copy-start.1) | copy-done | bytes 393240
  2.4 0.0 copy-start.2
  2.4 0.9 %copy-done.2 = s32[128,256]{1,0:T(8,128)S(1)} copy-done((s32[128,256]{1,0:T(8,128)S(1)}, s32[128,256]{1,0:T(8,128)}, u32[]{:S(2)}) %copy-start.2) | copy-done | bytes 131096
  3.3 0.2 pack_rows.1
  3.5 9.6 %collective-permute-start = (f32[16,16,256]{2,1,0:T(8,128)S(1)}, f32[16,16,256]{2,1,0:T(8,128)S(1)}, u32[]{:S(2)}, u32[]{:S(2)}) collective-permute-start(f32[16,16,256]{2,1,0:T(8,128)S(1)} %get-tuple-element.21), channel_id=1, source_target_pairs={{1,2},{2,1},{3,127},{5,6},{6,5},{7,123},{9,10},{10,9},{11,119},{13... | collective-permute-start | bytes 786440 | tf_op jit(solution)/shard_map/ppermute | solution.py:427
  13.1 0.1 collective-permute-start.1
  13.2 2.7 %extend.1 = (f32[16,176,128]{2,1,0:T(8,128)S(1)}, f32[16,176,128]{2,1,0:T(8,128)S(1)}, f32[16,176,128]{2,1,0:T(8,128)S(1)}, f32[2,160,128]{2,1,0:T(8,128)S(1)}, ...) custom-call(f32[12,128,256]{2,1,0:T(8,128)S(1)} %bitcast.3, f32[3,128,256]{2,1,0:T(8,128)S(1)} %copy-done.1, ...), custom_call_target="tpu_custom_call" | custom-call | tf_op jit(solution)/shard_map/extend/pallas_call | solution.py:171
  15.9 1.1 %collective-permute-done.ra = f32[16,16,256]{2,1,0:T(8,128)S(1)} collective-permute-done((f32[16,16,256]{2,1,0:T(8,128)S(1)}, f32[16,16,256]{2,1,0:T(8,128)S(1)}, u32[]{:S(2)}, u32[]{:S(2)}) %collective-permute-start) | collective-permute-done | bytes 262176 | tf_op jit(solution)/shard_map/ppermute | solution.py:427
  17.0 0.0 collective-permute-done.1.rb
  17.0 1.4 %halo_rows.1 = (f32[16,176,128]{2,1,0:T(8,128)S(1)}, f32[16,176,128]{2,1,0:T(8,128)S(1)}, f32[16,176,128]{2,1,0:T(8,128)S(1)}, f32[2,160,128]{2,1,0:T(8,128)S(1)}, f32[2,160,128]{2,1,0:T(8,128)S(1)}) custom-call(f32[16,16,256]{2,1,0:T(8,128)S(1)} %collective-permute-done.ra, ...), custom_call_target="tpu_custom_call", output_to_operand_aliasing={{0}: (2, {}), {1}: (3, {}), {2}: (4, {}), {3}: (5, {}), {4}... | custom-call | tf_op jit(solution)/shard_map/halo_rows/pallas_call | solution.py:189
  18.4 12.1 %interior.2.inner0 = f32[12,144,128]{2,1,0:T(8,128)S(1)} custom-call(f32[16,176,128]{2,1,0:T(8,128)S(1)} %get-tuple-element.32.tile, f32[176,128]{1,0:T(8,128)S(1)} %get-tuple-element.29.cor), custom_call_target="tpu_custom_call" | custom-call | tf_op jit(solution)/shard_map/interior/pallas_call | solution.py:339
  30.5 1.6 %collective-permute-start.2 = (f32[2,160,128]{2,1,0:T(8,128)S(1)}, f32[2,160,128]{2,1,0:T(8,128)S(1)}, u32[]{:S(2)}, u32[]{:S(2)}) collective-permute-start(f32[2,160,128]{2,1,0:T(8,128)S(1)} %get-tuple-element.33), channel_id=1, source_target_pairs={{0,4},{4,8},{8,12},{12,16},{16,20},{20,24},{24,28},{28,32},{32,36}... | collective-permute-start | bytes 491528 | tf_op jit(solution)/shard_map/ppermute | solution.py:433
  32.1 5.8 %collective-permute-start.3 = (f32[2,160,128]{2,1,0:T(8,128)S(1)}, f32[2,160,128]{2,1,0:T(8,128)S(1)}, u32[]{:S(2)}, u32[]{:S(2)}) collective-permute-start(f32[2,160,128]{2,1,0:T(8,128)S(1)} %get-tuple-element.34), channel_id=1, source_target_pairs={{4,0},{8,4},{12,8},{16,12},{20,16},{24,20},{28,24},{32,28},{36,32}... | collective-permute-start | bytes 491528 | tf_op jit(solution)/shard_map/ppermute | solution.py:434
  37.9 12.1 %interior.3.inner1 = f32[12,144,128]{2,1,0:T(8,128)S(1)} custom-call(f32[16,176,128]{2,1,0:T(8,128)S(1)} %get-tuple-element.36.tile, f32[176,128]{1,0:T(8,128)S(1)} %get-tuple-element.29.cor), custom_call_target="tpu_custom_call" | custom-call | tf_op jit(solution)/shard_map/interior/pallas_call | solution.py:339
  50.1 0.0 collective-permute-done.2.got_low
  50.1 0.0 collective-permute-done.3.got_high
  50.1 16.3 %edges.1 = f32[12,128,256]{2,1,0:T(8,128)} custom-call(f32[16,176,128]{2,1,0:T(8,128)S(1)} %get-tuple-element.28.start, f32[176,128]{1,0:T(8,128)S(1)} %get-tuple-element.29.cor, f32[2,160,128]{2,1,0:T(8,128)S(1)} %collective-permute-done.2.got_low, f32[2,160,128]{2,1,0:T(8,128)S(1)} %collective-permute-done.3.got_high, f32[12,144,128]{2,1,0:T(8,128)S(1)} %interior.2.inner0, ...), custom_call_target="tpu_custom_call" | custom-call | tf_op jit(solution)/shard_map/edges/pallas_call | solution.py:390
Async XLA Ops:
  0.0 1.4 %copy-start = (f32[4,3,128,256]{3,2,1,0:T(8,128)S(1)}, f32[4,3,128,256]{3,2,1,0:T(8,128)}, u32[]{:S(2)}) copy-start(f32[4,3,128,256]{3,2,1,0:T(8,128)} %param.3) | copy-start | bytes 4718596
  1.4 1.0 %copy-start.1 = (f32[3,128,256]{2,1,0:T(8,128)S(1)}, f32[3,128,256]{2,1,0:T(8,128)}, u32[]{:S(2)}) copy-start(f32[3,128,256]{2,1,0:T(8,128)} %m_all.1) | copy-start | bytes 1179652
  2.4 0.9 %copy-start.2 = (s32[128,256]{1,0:T(8,128)S(1)}, s32[128,256]{1,0:T(8,128)}, u32[]{:S(2)}) copy-start(s32[128,256]{1,0:T(8,128)} %w_all.1) | copy-start | bytes 393220
  3.5 13.5 %collective-permute-start = (f32[16,16,256]{2,1,0:T(8,128)S(1)}, f32[16,16,256]{2,1,0:T(8,128)S(1)}, u32[]{:S(2)}, u32[]{:S(2)}) collective-permute-start(f32[16,16,256]{2,1,0:T(8,128)S(1)} %get-tuple-element.21), channel_id=1, source_target_pairs={{1,2},{2,1},{3,127},{5,6},{6,5},{7,123},{9,10},{10,9},{11,119},{13... | collective-permute-start | bytes 786440 | tf_op jit(solution)/shard_map/ppermute | solution.py:427
  13.1 3.9 %collective-permute-start.1 = (f32[16,16,256]{2,1,0:T(8,128)S(1)}, f32[16,16,256]{2,1,0:T(8,128)S(1)}, u32[]{:S(2)}, u32[]{:S(2)}) collective-permute-start(f32[16,16,256]{2,1,0:T(8,128)S(1)} %get-tuple-element.22), channel_id=1, source_target_pairs={{0,1},{1,0},{2,3},{3,2},{4,5},{5,4},{6,7},{7,6},{8,9},{9,8},{10,11... | collective-permute-start | bytes 786440 | tf_op jit(solution)/shard_map/ppermute | solution.py:428
  30.5 19.5 %collective-permute-start.2 = (f32[2,160,128]{2,1,0:T(8,128)S(1)}, f32[2,160,128]{2,1,0:T(8,128)S(1)}, u32[]{:S(2)}, u32[]{:S(2)}) collective-permute-start(f32[2,160,128]{2,1,0:T(8,128)S(1)} %get-tuple-element.33), channel_id=1, source_target_pairs={{0,4},{4,8},{8,12},{12,16},{16,20},{20,24},{24,28},{28,32},{32,36}... | collective-permute-start | bytes 491528 | tf_op jit(solution)/shard_map/ppermute | solution.py:433
  32.1 18.0 %collective-permute-start.3 = (f32[2,160,128]{2,1,0:T(8,128)S(1)}, f32[2,160,128]{2,1,0:T(8,128)S(1)}, u32[]{:S(2)}, u32[]{:S(2)}) collective-permute-start(f32[2,160,128]{2,1,0:T(8,128)S(1)} %get-tuple-element.34), channel_id=1, source_target_pairs={{4,0},{8,4},{12,8},{16,12},{20,16},{24,20},{28,24},{32,28},{36,32}... | collective-permute-start | bytes 491528 | tf_op jit(solution)/shard_map/ppermute | solution.py:434

commit v3 on v2

--- a/solution.py
+++ b/solution.py
@@ -91,18 +91,19 @@
             tiles[0][p, here] = lo
             tiles[1][p, here] = jnp.where(lane < 96, hi, lo)
             tiles[2][p, here] = jnp.where(lane < 64, shifted(lo, 32), hi)
-            mine = jnp.logical_and(lane >= 16 * q, lane < 16 * q + 16)
-            low = jnp.where(mine, shifted(lo, 16 * q), low)
-            high = jnp.where(mine, shifted(hi, 16 * q - 112), high)
+            slot = 16 * ((q + 1) % 8)
+            low = jnp.where(jnp.logical_and(lane >= 16 * q, lane < 16 * q + 16), shifted(lo, 16 * q), low)
+            high = jnp.where(jnp.logical_and(lane >= slot, lane < slot + 16), shifted(hi, slot - 112), high)
         send_low[group, pl.ds(at, 8)] = low
         send_high[group, pl.ds(at, 8)] = high
 
 
-def extend_kernel(x_all, m_all, w_all, tile0, tile1, tile2, send_low, send_high, cor, x, m, w, sems):
+def extend_kernel(x_all, m_all, w_all, tile0, tile1, tile2, send_low, send_high, cor, weights, x, m, w, sems):
     pairs = ((x_all, x), (m_all, m), (w_all, w))
     copies = [pltpu.make_async_copy(a, b, sems.at[i]) for i, (a, b) in enumerate(pairs)]
     for copy in copies:
         copy.start()
+    weights[...] = line_weights()
     lat = lax.axis_index("lat")
     block = x.shape[1]
     total = block * lax.axis_size("lat")
@@ -171,8 +172,16 @@
     return pl.pallas_call(
         extend_kernel,
         in_specs=[pl.BlockSpec(memory_space=pltpu.HBM)] * 3,
-        out_specs=[vmem] * 6,
-        out_shape=[tile, tile, tile, send, send, jax.ShapeDtypeStruct((span + 2 * PAD, LANES), f32)],
+        out_specs=[vmem] * 7,
+        out_shape=[
+            tile,
+            tile,
+            tile,
+            send,
+            send,
+            jax.ShapeDtypeStruct((span + 2 * PAD, LANES), f32),
+            jax.ShapeDtypeStruct((2 * LANES, 4 * LANES), jnp.bfloat16),
+        ],
         scratch_shapes=[
             pltpu.VMEM(x.shape, f32),
             pltpu.VMEM(mixing.shape, f32),
@@ -314,8 +323,9 @@
         start = PAD + 2 * (s + 1) - spare
         dst = out if s == STEPS - 1 else (even if s % 2 == 0 else odd)
         dst_start = PAD - spare if s == STEPS - 1 else start
-        first = start // 16 * 16
-        count = -(-(start + 8 * span) // 16) * 16 - first
+        lowest = PAD + 2 * (s + 1)
+        first = lowest // 8 * 8
+        count = -(-(lowest + need - first) // 16) * 16
         products(src, weights, prod, first, count)
 
         def coef(p, t, start=start, span=span):
@@ -326,54 +336,54 @@
         src = dst
 
 
-def interior_kernel(seam, tile, cor, out, even, odd, weights, prod):
-    weights[...] = line_weights()
+def interior_kernel(seam, tile, cor, weights, out, even, odd, prod):
     window(tile, cor, (seam,), weights, prod, even, odd, out)
 
 
-def interior(tile, cor, seam):
+def interior(tile, cor, weights, seam):
     rows = tile.shape[1]
     block = rows - 2 * PAD - 2 * HALO
     vmem = pl.BlockSpec(memory_space=pltpu.VMEM)
     f32 = jnp.float32
     return pl.pallas_call(
         functools.partial(interior_kernel, seam),
-        in_specs=[vmem, vmem],
+        in_specs=[vmem] * 3,
         out_specs=vmem,
         out_shape=jax.ShapeDtypeStruct((STATE, block + 2 * PAD, LANES), f32),
         scratch_shapes=[
             pltpu.VMEM((STATE, rows, LANES), f32),
             pltpu.VMEM((STATE, rows, LANES), f32),
-            pltpu.VMEM((2 * LANES, 4 * LANES), jnp.bfloat16),
             pltpu.VMEM((4, STATE, rows, LANES), f32),
         ],
         compiler_params=params(),
         name="interior",
-    )(tile, cor)
-
-
-def edge_kernel(start, cor, got_low, got_high, inner0, inner1, out, tile, even, odd, edge, weights, prod):
+    )(tile, cor, weights)
+
+
+def edge_kernel(start, cor, weights, got_low, got_high, inner0, inner1, result, tile, even, odd, edge, prod, out, sems):
     span = got_low.shape[1]
-    block = out.shape[1]
-    weights[...] = line_weights()
+    block = result.shape[1]
 
     @pl.loop(0, span // 8)
     def _(g):
         r = pl.multiple_of(g * 8, 8)
         lane = lax.broadcasted_iota(jnp.int32, (8, LANES), 1)
         for p in range(PLANES):
-            left = shifted(got_low[p // 8, pl.ds(r, 8)], 16 - 16 * (p % 8))
-            right = shifted(got_high[p // 8, pl.ds(r, 8)], -16 * (p % 8))
+            q = p % 8
+            mine = jnp.logical_and(lane >= 16 * q, lane < 16 * q + 16)
+            both = jnp.where(mine, got_high[p // 8, pl.ds(r, 8)], got_low[p // 8, pl.ds(r, 8)])
             mid = start[p, pl.ds(PAD + r, 8)]
-            tile[p, pl.ds(PAD + r, 8)] = jnp.where(lane < 16, right, jnp.where(lane < 32, left, mid))
+            tile[p, pl.ds(PAD + r, 8)] = jnp.where(lane < 32, shifted(both, -16 * q), mid)
 
     window(tile, cor, (16, 64), weights, prod, even, odd, edge)
 
-    @pl.loop(0, block // 8)
-    def _(g):
-        r = pl.multiple_of(g * 8, 8)
-        lane = lax.broadcasted_iota(jnp.int32, (8, LANES), 1)
-        for p in range(STATE):
+    copies = []
+    for p in range(STATE):
+
+        @pl.loop(0, block // 8, unroll=4)
+        def _(g, p=p):
+            r = pl.multiple_of(g * 8, 8)
+            lane = lax.broadcasted_iota(jnp.int32, (8, LANES), 1)
             here = pl.ds(PAD + r, 8)
             e = edge[p, here]
             lo = inner0[p, here]
@@ -381,28 +391,34 @@
             out[p, pl.ds(r, 8), :LANES] = jnp.where(lane < 16, shifted(e, -32), jnp.where(lane < 112, lo, hi))
             out[p, pl.ds(r, 8), LANES:] = jnp.where(lane < 80, hi, e)
 
-
-def edges(start, cor, got_low, got_high, inner0, inner1):
+        copies.append(pltpu.make_async_copy(out.at[p], result.at[p], sems.at[p]))
+        copies[-1].start()
+    for copy in copies:
+        copy.wait()
+
+
+def edges(start, cor, weights, got_low, got_high, inner0, inner1):
     rows = start.shape[1]
     block = rows - 2 * PAD - 2 * HALO
     f32 = jnp.float32
     vmem = pl.BlockSpec(memory_space=pltpu.VMEM)
     return pl.pallas_call(
         edge_kernel,
-        in_specs=[vmem] * 6,
-        out_specs=vmem,
+        in_specs=[vmem] * 7,
+        out_specs=pl.BlockSpec(memory_space=pltpu.HBM),
         out_shape=jax.ShapeDtypeStruct((STATE, block, 2 * LANES), f32),
         scratch_shapes=[
             pltpu.VMEM((PLANES, rows, LANES), f32),
             pltpu.VMEM((STATE, rows, LANES), f32),
             pltpu.VMEM((STATE, rows, LANES), f32),
             pltpu.VMEM((STATE, block + 2 * PAD, LANES), f32),
-            pltpu.VMEM((2 * LANES, 4 * LANES), jnp.bfloat16),
             pltpu.VMEM((4, STATE, rows, LANES), f32),
+            pltpu.VMEM((STATE, block, 2 * LANES), f32),
+            pltpu.SemaphoreType.DMA((STATE,)),
         ],
         compiler_params=params(),
         name="edges",
-    )(start, cor, got_low, got_high, inner0, inner1)
+    )(start, cor, weights, got_low, got_high, inner0, inner1)
 
 
 def body(ocean_state, mixing, land_sea):
@@ -423,17 +439,18 @@
     west = [((i + 1) % n_lon, i) for i in range(n_lon)]
 
     x = ocean_state.reshape(STATE, block, cols)
+    x, mixing, land_sea = (pltpu.with_memory_space_constraint(v, pltpu.HBM) for v in (x, mixing, land_sea))
     to_a, to_b = pack_rows(x, mixing, land_sea)
     ra = lax.ppermute(to_a, axes, pairs_a)
     rb = lax.ppermute(to_b, axes, pairs_b)
-    *parts, cor = extend(x, mixing, land_sea)
+    *parts, cor, weights = extend(x, mixing, land_sea)
     tile0, tile1, tile2, send_low, send_high = halo_rows(ra, rb, *parts)
-    inner0 = interior(tile0, cor, 0)
+    inner0 = interior(tile0, cor, weights, 0)
     send_low, send_high, inner0 = lax.optimization_barrier((send_low, send_high, inner0))
     got_low = lax.ppermute(send_high, "lon", east)
     got_high = lax.ppermute(send_low, "lon", west)
-    inner1 = interior(tile1, cor, 96)
-    out = edges(tile2, cor, got_low, got_high, inner0, inner1)
+    inner1 = interior(tile1, cor, weights, 96)
+    out = edges(tile2, cor, weights, got_low, got_high, inner0, inner1)
     return out.reshape(ocean_state.shape)
 
 

time: 66.6 us -> 63.8 us (0.958)
  local copies, waits for them, and re-layouts: 3.31 us -> 0 us
  Pallas kernels: 44.9 us -> 45.9 us
  waiting for transfers between devices: 1.06 us -> 0.38 us
    unnamed x6 -> x0, local copies, waits for them, and re-layouts: 3.31 us -> none
    pallas_call x1, Pallas kernels: 0.21 us -> 1.12 us  [pack_rows(): pl.pallas_call(pack_rows_kernel, in_specs=[pl.BlockSpec(memory_space=pltp...]
    pallas_call x1, Pallas kernels: 2.7 us -> 3.39 us  [extend(): pl.pallas_call(extend_kernel, in_specs=[pl.BlockSpec(memory_space=pltpu.H...]
    ppermute x1, waiting for transfers between devices: 1.06 us -> 0.37 us  [body(): ra = lax.ppermute(to_a, axes, pairs_a)]
  transfers between devices with their start and end apart: 4 -> 4, of which waited for: 1 -> 1; matrix products, arithmetic and copies ran while one was open for 0% -> 0% of each run, Pallas kernels for 22% -> 23%
where the time goes in v3:
time: 63.8 us; the launch traced here: 63.6 us
  Pallas kernels  45.9 us (72%)
  starting transfers between devices  17.1 us (27%)
    pallas_call x2, Pallas kernels, interior(): pl.pallas_call(functools.partial(interior_kernel, seam), in_specs=[vmem]...  22.7 us
    pallas_call x1, Pallas kernels, edges(): pl.pallas_call(edge_kernel, in_specs=[vmem] * 7, out_specs=pl.BlockSpec(m...  17.3 us
    ppermute x1, starting transfers between devices, body(): ra = lax.ppermute(to_a, axes, pairs_a)  9.59 us
    ppermute x1, starting transfers between devices, body(): got_high = lax.ppermute(send_low, 'lon', west)  5.85 us
    pallas_call x1, Pallas kernels, extend(): pl.pallas_call(extend_kernel, in_specs=[pl.BlockSpec(memory_space=pltpu.H...  3.39 us
    ppermute x1, starting transfers between devices, body(): got_low = lax.ppermute(send_high, 'lon', east)  1.55 us
    pallas_call x1, Pallas kernels, halo_rows(): pl.pallas_call(halo_rows_kernel, in_specs=[vmem] * 7, out_specs=[vmem] *...  1.38 us
  transfers between devices with their start and end apart: 4, of which 1 were waited for; matrix products, arithmetic and copies ran while one was open for 0% of the time, Pallas kernels for 23%

profile of v3, /device:TPU:9, one launch (start us, length us, event | category | flops | bytes accessed | tf_op | source)
XLA Modules:
  0.0 63.6 jit_solution(11771188987742743468)
XLA Ops:
  0.0 1.1 %pack_rows.1 = (f32[16,16,256]{2,1,0:T(8,128)S(1)}, f32[16,16,256]{2,1,0:T(8,128)S(1)}) custom-call(f32[12,128,256]{2,1,0:T(8,128)} %bitcast.2, f32[3,128,256]{2,1,0:T(8,128)} %m_all.1, s32[128,256]{1,0:T(8,128)} %w_all.1), custom_call_target="tpu_custom_call" | custom-call | tf_op jit(solution)/shard_map/pack_rows/pallas_call | solution.py:55
  1.1 9.6 %collective-permute-start = (f32[16,16,256]{2,1,0:T(8,128)S(1)}, f32[16,16,256]{2,1,0:T(8,128)S(1)}, u32[]{:S(2)}, u32[]{:S(2)}) collective-permute-start(f32[16,16,256]{2,1,0:T(8,128)S(1)} %get-tuple-element.22), channel_id=1, source_target_pairs={{1,2},{2,1},{3,127},{5,6},{6,5},{7,123},{9,10},{10,9},{11,119},{13... | collective-permute-start | bytes 786440 | tf_op jit(solution)/shard_map/ppermute | solution.py:444
  10.7 0.1 collective-permute-start.1
  10.8 3.4 %extend.1 = (f32[16,176,128]{2,1,0:T(8,128)S(1)}, f32[16,176,128]{2,1,0:T(8,128)S(1)}, f32[16,176,128]{2,1,0:T(8,128)S(1)}, f32[2,160,128]{2,1,0:T(8,128)S(1)}, ...) custom-call(f32[12,128,256]{2,1,0:T(8,128)} %bitcast.3, f32[3,128,256]{2,1,0:T(8,128)} %m_all.1, ...), custom_call_target="tpu_custom_call" | custom-call | tf_op jit(solution)/shard_map/extend/pallas_call | solution.py:172
  14.2 0.4 collective-permute-done.ra
  14.6 0.0 collective-permute-done.1.rb
  14.6 1.4 %halo_rows.1 = (f32[16,176,128]{2,1,0:T(8,128)S(1)}, f32[16,176,128]{2,1,0:T(8,128)S(1)}, f32[16,176,128]{2,1,0:T(8,128)S(1)}, f32[2,160,128]{2,1,0:T(8,128)S(1)}, f32[2,160,128]{2,1,0:T(8,128)S(1)}) custom-call(f32[16,16,256]{2,1,0:T(8,128)S(1)} %collective-permute-done.ra, ...), custom_call_target="tpu_custom_call", output_to_operand_aliasing={{0}: (2, {}), {1}: (3, {}), {2}: (4, {}), {3}: (5, {}), {4}... | custom-call | tf_op jit(solution)/shard_map/halo_rows/pallas_call | solution.py:198
  16.0 11.4 %interior.2.inner0 = f32[12,144,128]{2,1,0:T(8,128)S(1)} custom-call(f32[16,176,128]{2,1,0:T(8,128)S(1)} %get-tuple-element.34.tile, f32[176,128]{1,0:T(8,128)S(1)} %get-tuple-element.30.cor, bf16[256,512]{1,0:T(8,128)(2,1)S(1)} %get-tuple-element.31.weights), custom_call_target="tpu_custom_call" | custom-call | tf_op jit(solution)/shard_map/interior/pallas_call | solution.py:348
  27.4 1.6 %collective-permute-start.2 = (f32[2,160,128]{2,1,0:T(8,128)S(1)}, f32[2,160,128]{2,1,0:T(8,128)S(1)}, u32[]{:S(2)}, u32[]{:S(2)}) collective-permute-start(f32[2,160,128]{2,1,0:T(8,128)S(1)} %get-tuple-element.35), channel_id=1, source_target_pairs={{0,4},{4,8},{8,12},{12,16},{16,20},{20,24},{24,28},{28,32},{32,36}... | collective-permute-start | bytes 491528 | tf_op jit(solution)/shard_map/ppermute | solution.py:450
  28.9 5.9 %collective-permute-start.3 = (f32[2,160,128]{2,1,0:T(8,128)S(1)}, f32[2,160,128]{2,1,0:T(8,128)S(1)}, u32[]{:S(2)}, u32[]{:S(2)}) collective-permute-start(f32[2,160,128]{2,1,0:T(8,128)S(1)} %get-tuple-element.36), channel_id=1, source_target_pairs={{4,0},{8,4},{12,8},{16,12},{20,16},{24,20},{28,24},{32,28},{36,32}... | collective-permute-start | bytes 491528 | tf_op jit(solution)/shard_map/ppermute | solution.py:451
  34.8 11.4 %interior.3.inner1 = f32[12,144,128]{2,1,0:T(8,128)S(1)} custom-call(f32[16,176,128]{2,1,0:T(8,128)S(1)} %get-tuple-element.38.tile, f32[176,128]{1,0:T(8,128)S(1)} %get-tuple-element.30.cor, bf16[256,512]{1,0:T(8,128)(2,1)S(1)} %get-tuple-element.31.weights), custom_call_target="tpu_custom_call" | custom-call | tf_op jit(solution)/shard_map/interior/pallas_call | solution.py:348
  46.1 0.0 collective-permute-done.2.got_low
  46.1 0.0 collective-permute-done.3.got_high
  46.1 17.3 %edges.1 = f32[12,128,256]{2,1,0:T(8,128)} custom-call(f32[16,176,128]{2,1,0:T(8,128)S(1)} %get-tuple-element.29.start, f32[176,128]{1,0:T(8,128)S(1)} %get-tuple-element.30.cor, bf16[256,512]{1,0:T(8,128)(2,1)S(1)} %get-tuple-element.31.weights, f32[2,160,128]{2,1,0:T(8,128)S(1)} %collective-permute-done.2.got_low, ...), custom_call_target="tpu_custom_call" | custom-call | tf_op jit(solution)/shard_map/edges/pallas_call | solution.py:405
Async XLA Ops:
  1.1 13.5 %collective-permute-start = (f32[16,16,256]{2,1,0:T(8,128)S(1)}, f32[16,16,256]{2,1,0:T(8,128)S(1)}, u32[]{:S(2)}, u32[]{:S(2)}) collective-permute-start(f32[16,16,256]{2,1,0:T(8,128)S(1)} %get-tuple-element.22), channel_id=1, source_target_pairs={{1,2},{2,1},{3,127},{5,6},{6,5},{7,123},{9,10},{10,9},{11,119},{13... | collective-permute-start | bytes 786440 | tf_op jit(solution)/shard_map/ppermute | solution.py:444
  10.7 3.9 %collective-permute-start.1 = (f32[16,16,256]{2,1,0:T(8,128)S(1)}, f32[16,16,256]{2,1,0:T(8,128)S(1)}, u32[]{:S(2)}, u32[]{:S(2)}) collective-permute-start(f32[16,16,256]{2,1,0:T(8,128)S(1)} %get-tuple-element.23), channel_id=1, source_target_pairs={{0,1},{1,0},{2,3},{3,2},{4,5},{5,4},{6,7},{7,6},{8,9},{9,8},{10,11... | collective-permute-start | bytes 786440 | tf_op jit(solution)/shard_map/ppermute | solution.py:445
  27.4 18.8 %collective-permute-start.2 = (f32[2,160,128]{2,1,0:T(8,128)S(1)}, f32[2,160,128]{2,1,0:T(8,128)S(1)}, u32[]{:S(2)}, u32[]{:S(2)}) collective-permute-start(f32[2,160,128]{2,1,0:T(8,128)S(1)} %get-tuple-element.35), channel_id=1, source_target_pairs={{0,4},{4,8},{8,12},{12,16},{16,20},{20,24},{24,28},{28,32},{32,36}... | collective-permute-start | bytes 491528 | tf_op jit(solution)/shard_map/ppermute | solution.py:450
  28.9 17.2 %collective-permute-start.3 = (f32[2,160,128]{2,1,0:T(8,128)S(1)}, f32[2,160,128]{2,1,0:T(8,128)S(1)}, u32[]{:S(2)}, u32[]{:S(2)}) collective-permute-start(f32[2,160,128]{2,1,0:T(8,128)S(1)} %get-tuple-element.36), channel_id=1, source_target_pairs={{4,0},{8,4},{12,8},{16,12},{20,16},{24,20},{28,24},{32,28},{36,32}... | collective-permute-start | bytes 491528 | tf_op jit(solution)/shard_map/ppermute | solution.py:451

commit v4 on v3

--- a/solution.py
+++ b/solution.py
@@ -75,8 +75,16 @@
     a = lax.broadcasted_iota(jnp.int32, (cols, cols), 0)
     b = lax.broadcasted_iota(jnp.int32, (cols, cols), 1)
     right = jnp.where(a + b == cols - 1, 1.0, 0.0).astype(jnp.float32)
-    dot = functools.partial(jnp.dot, precision=lax.Precision.HIGHEST, preferred_element_type=jnp.float32)
-    return dot(dot(left, flat), right).reshape(slab.shape)
+    left, right = left.astype(jnp.bfloat16), right.astype(jnp.bfloat16)
+    out = None
+    rest = flat
+    for _ in range(3):
+        part = rest.astype(jnp.bfloat16)
+        rest = rest - part.astype(jnp.float32)
+        turned = jnp.dot(left, part, preferred_element_type=jnp.float32).astype(jnp.bfloat16)
+        turned = jnp.dot(turned, right, preferred_element_type=jnp.float32)
+        out = turned if out is None else out + turned
+    return out.reshape(slab.shape)
 
 
 def place(at, source, tiles, send_low, send_high):
@@ -239,7 +247,7 @@
             prod[j, planes, rows, :] = got[:, j * LANES : (j + 1) * LANES].reshape(K, count, LANES)
 
 
-def substep(src, dst, coef, cor, prod, mask, start, dst_start, span, unroll=2):
+def substep(src, dst, coef, cor, prod, mask, start, dst_start, span, unroll=3):
     def load(ref, p, t):
         return ref[p, pl.ds(start + t, 8, stride=span), :]
 
@@ -301,7 +309,7 @@
                     new = new + (wet_cor * load(src, p + K, t) - wet * grad_lon)
                 if f == 3:
                     new = new - (wet_cor * load(src, p - K, t) + wet * (p_next[k] - p_prev[k]))
-                dst[p, pl.ds(dst_start + t, 8, stride=span), :] = new
+                dst(p, pl.ds(dst_start + t, 8, stride=span), new)
         return above, p_here, p_next
 
     init = (fluxes(-1), pressures(-1), pressures(0))
@@ -321,7 +329,12 @@
         need = span_rows - 4 * (s + 1)
         spare = (8 * span - need) // 2
         start = PAD + 2 * (s + 1) - spare
-        dst = out if s == STEPS - 1 else (even if s % 2 == 0 else odd)
+        keep = even if s % 2 == 0 else odd
+
+        def put(p, rows, new, keep=keep):
+            keep[p, rows, :] = new
+
+        dst = out if s == STEPS - 1 else put
         dst_start = PAD - spare if s == STEPS - 1 else start
         lowest = PAD + 2 * (s + 1)
         first = lowest // 8 * 8
@@ -333,11 +346,14 @@
 
         mask = jnp.where(room >= 2 * (s + 1), 1.0, 0.0)
         substep(src, dst, coef, cor, prod, mask, start, dst_start, span)
-        src = dst
+        src = keep
 
 
 def interior_kernel(seam, tile, cor, weights, out, even, odd, prod):
-    window(tile, cor, (seam,), weights, prod, even, odd, out)
+    def put(p, rows, new):
+        out[p, rows, :] = new
+
+    window(tile, cor, (seam,), weights, prod, even, odd, put)
 
 
 def interior(tile, cor, weights, seam):
@@ -360,11 +376,11 @@
     )(tile, cor, weights)
 
 
-def edge_kernel(start, cor, weights, got_low, got_high, inner0, inner1, result, tile, even, odd, edge, prod, out, sems):
+def edge_kernel(start, cor, weights, got_low, got_high, inner0, inner1, result, tile, even, odd, prod, out_low, out_high, sems):
     span = got_low.shape[1]
     block = result.shape[1]
 
-    @pl.loop(0, span // 8)
+    @pl.loop(0, span // 8, unroll=4)
     def _(g):
         r = pl.multiple_of(g * 8, 8)
         lane = lax.broadcasted_iota(jnp.int32, (8, LANES), 1)
@@ -375,24 +391,20 @@
             mid = start[p, pl.ds(PAD + r, 8)]
             tile[p, pl.ds(PAD + r, 8)] = jnp.where(lane < 32, shifted(both, -16 * q), mid)
 
-    window(tile, cor, (16, 64), weights, prod, even, odd, edge)
-
+    def put(p, rows, new):
+        lane = lax.broadcasted_iota(jnp.int32, (8, LANES), 1)
+        lo = inner0[p, rows, :]
+        hi = inner1[p, rows, :]
+        out_low[p, rows, :] = jnp.where(lane < 16, shifted(new, -32), jnp.where(lane < 112, lo, hi))
+        out_high[p, rows, :] = jnp.where(lane < 80, hi, new)
+
+    window(tile, cor, (16, 64), weights, prod, even, odd, put)
     copies = []
-    for p in range(STATE):
-
-        @pl.loop(0, block // 8, unroll=4)
-        def _(g, p=p):
-            r = pl.multiple_of(g * 8, 8)
-            lane = lax.broadcasted_iota(jnp.int32, (8, LANES), 1)
-            here = pl.ds(PAD + r, 8)
-            e = edge[p, here]
-            lo = inner0[p, here]
-            hi = inner1[p, here]
-            out[p, pl.ds(r, 8), :LANES] = jnp.where(lane < 16, shifted(e, -32), jnp.where(lane < 112, lo, hi))
-            out[p, pl.ds(r, 8), LANES:] = jnp.where(lane < 80, hi, e)
-
-        copies.append(pltpu.make_async_copy(out.at[p], result.at[p], sems.at[p]))
-        copies[-1].start()
+    for i, half in enumerate((out_low, out_high)):
+        source = half.at[:, pl.ds(PAD, block), :]
+        copies.append(pltpu.make_async_copy(source, result.at[:, :, pl.ds(i * LANES, LANES)], sems.at[i]))
+    for copy in copies:
+        copy.start()
     for copy in copies:
         copy.wait()
 
@@ -411,10 +423,10 @@
             pltpu.VMEM((PLANES, rows, LANES), f32),
             pltpu.VMEM((STATE, rows, LANES), f32),
             pltpu.VMEM((STATE, rows, LANES), f32),
+            pltpu.VMEM((4, STATE, rows, LANES), f32),
             pltpu.VMEM((STATE, block + 2 * PAD, LANES), f32),
-            pltpu.VMEM((4, STATE, rows, LANES), f32),
-            pltpu.VMEM((STATE, block, 2 * LANES), f32),
-            pltpu.SemaphoreType.DMA((STATE,)),
+            pltpu.VMEM((STATE, block + 2 * PAD, LANES), f32),
+            pltpu.SemaphoreType.DMA((2,)),
         ],
         compiler_params=params(),
         name="edges",

time: 63.8 us -> 59.8 us (0.937)
  Pallas kernels: 45.9 us -> 41.9 us
    pallas_call x1, Pallas kernels: 17.3 us -> 13.7 us  [edges(): pl.pallas_call(edge_kernel, in_specs=[vmem] * 7, out_specs=pl.BlockSpec(m...]
  transfers between devices with their start and end apart: 4 -> 4, of which waited for: 1 -> 1; matrix products, arithmetic and copies ran while one was open for 0% -> 0% of each run, Pallas kernels for 23% -> 25%
where the time goes in v4:
time: 59.8 us; the launch traced here: 59.6 us
  Pallas kernels  41.9 us (70%)
  starting transfers between devices  17.1 us (29%)
    pallas_call x2, Pallas kernels, interior(): pl.pallas_call(functools.partial(interior_kernel, seam), in_specs=[vmem]...  22.8 us
    pallas_call x1, Pallas kernels, edges(): pl.pallas_call(edge_kernel, in_specs=[vmem] * 7, out_specs=pl.BlockSpec(m...  13.7 us
    ppermute x1, starting transfers between devices, body(): ra = lax.ppermute(to_a, axes, pairs_a)  9.59 us
    ppermute x1, starting transfers between devices, body(): got_high = lax.ppermute(send_low, 'lon', west)  5.83 us
    pallas_call x1, Pallas kernels, extend(): pl.pallas_call(extend_kernel, in_specs=[pl.BlockSpec(memory_space=pltpu.H...  3.39 us
    ppermute x1, starting transfers between devices, body(): got_low = lax.ppermute(send_high, 'lon', east)  1.57 us
  transfers between devices with their start and end apart: 4, of which 1 were waited for; matrix products, arithmetic and copies ran while one was open for 0% of the time, Pallas kernels for 25%

profile of v4, /device:TPU:9, one launch (start us, length us, event | category | flops | bytes accessed | tf_op | source)
XLA Modules:
  0.0 59.6 jit_solution(18003937029985678832)
XLA Ops:
  0.0 1.1 %pack_rows.1 = (f32[16,16,256]{2,1,0:T(8,128)S(1)}, f32[16,16,256]{2,1,0:T(8,128)S(1)}) custom-call(f32[12,128,256]{2,1,0:T(8,128)} %bitcast.2, f32[3,128,256]{2,1,0:T(8,128)} %m_all.1, s32[128,256]{1,0:T(8,128)} %w_all.1), custom_call_target="tpu_custom_call" | custom-call | tf_op jit(solution)/shard_map/pack_rows/pallas_call | solution.py:55
  1.1 9.6 %collective-permute-start = (f32[16,16,256]{2,1,0:T(8,128)S(1)}, f32[16,16,256]{2,1,0:T(8,128)S(1)}, u32[]{:S(2)}, u32[]{:S(2)}) collective-permute-start(f32[16,16,256]{2,1,0:T(8,128)S(1)} %get-tuple-element.22), channel_id=1, source_target_pairs={{1,2},{2,1},{3,127},{5,6},{6,5},{7,123},{9,10},{10,9},{11,119},{13... | collective-permute-start | bytes 786440 | tf_op jit(solution)/shard_map/ppermute | solution.py:456
  10.7 0.1 collective-permute-start.1
  10.8 3.4 %extend.1 = (f32[16,176,128]{2,1,0:T(8,128)S(1)}, f32[16,176,128]{2,1,0:T(8,128)S(1)}, f32[16,176,128]{2,1,0:T(8,128)S(1)}, f32[2,160,128]{2,1,0:T(8,128)S(1)}, ...) custom-call(f32[12,128,256]{2,1,0:T(8,128)} %bitcast.3, f32[3,128,256]{2,1,0:T(8,128)} %m_all.1, ...), custom_call_target="tpu_custom_call" | custom-call | tf_op jit(solution)/shard_map/extend/pallas_call | solution.py:180
  14.2 0.4 collective-permute-done.ra
  14.6 0.0 collective-permute-done.1.rb
  14.6 0.9 %halo_rows.1 = (f32[16,176,128]{2,1,0:T(8,128)S(1)}, f32[16,176,128]{2,1,0:T(8,128)S(1)}, f32[16,176,128]{2,1,0:T(8,128)S(1)}, f32[2,160,128]{2,1,0:T(8,128)S(1)}, f32[2,160,128]{2,1,0:T(8,128)S(1)}) custom-call(f32[16,16,256]{2,1,0:T(8,128)S(1)} %collective-permute-done.ra, ...), custom_call_target="tpu_custom_call", output_to_operand_aliasing={{0}: (2, {}), {1}: (3, {}), {2}: (4, {}), {3}: (5, {}), {4}... | custom-call | tf_op jit(solution)/shard_map/halo_rows/pallas_call | solution.py:206
  15.5 11.4 %interior.2.inner0 = f32[12,144,128]{2,1,0:T(8,128)S(1)} custom-call(f32[16,176,128]{2,1,0:T(8,128)S(1)} %get-tuple-element.34.tile, f32[176,128]{1,0:T(8,128)S(1)} %get-tuple-element.30.cor, bf16[256,512]{1,0:T(8,128)(2,1)S(1)} %get-tuple-element.31.weights), custom_call_target="tpu_custom_call" | custom-call | tf_op jit(solution)/shard_map/interior/pallas_call | solution.py:364
  26.9 1.6 %collective-permute-start.2 = (f32[2,160,128]{2,1,0:T(8,128)S(1)}, f32[2,160,128]{2,1,0:T(8,128)S(1)}, u32[]{:S(2)}, u32[]{:S(2)}) collective-permute-start(f32[2,160,128]{2,1,0:T(8,128)S(1)} %get-tuple-element.35), channel_id=1, source_target_pairs={{0,4},{4,8},{8,12},{12,16},{16,20},{20,24},{24,28},{28,32},{32,36}... | collective-permute-start | bytes 491528 | tf_op jit(solution)/shard_map/ppermute | solution.py:462
  28.5 5.8 %collective-permute-start.3 = (f32[2,160,128]{2,1,0:T(8,128)S(1)}, f32[2,160,128]{2,1,0:T(8,128)S(1)}, u32[]{:S(2)}, u32[]{:S(2)}) collective-permute-start(f32[2,160,128]{2,1,0:T(8,128)S(1)} %get-tuple-element.36), channel_id=1, source_target_pairs={{4,0},{8,4},{12,8},{16,12},{20,16},{24,20},{28,24},{32,28},{36,32}... | collective-permute-start | bytes 491528 | tf_op jit(solution)/shard_map/ppermute | solution.py:463
  34.3 11.4 %interior.3.inner1 = f32[12,144,128]{2,1,0:T(8,128)S(1)} custom-call(f32[16,176,128]{2,1,0:T(8,128)S(1)} %get-tuple-element.38.tile, f32[176,128]{1,0:T(8,128)S(1)} %get-tuple-element.30.cor, bf16[256,512]{1,0:T(8,128)(2,1)S(1)} %get-tuple-element.31.weights), custom_call_target="tpu_custom_call" | custom-call | tf_op jit(solution)/shard_map/interior/pallas_call | solution.py:364
  45.7 0.0 collective-permute-done.2.got_low
  45.7 0.0 collective-permute-done.3.got_high
  45.7 13.7 %edges.1 = f32[12,128,256]{2,1,0:T(8,128)} custom-call(f32[16,176,128]{2,1,0:T(8,128)S(1)} %get-tuple-element.29.start, f32[176,128]{1,0:T(8,128)S(1)} %get-tuple-element.30.cor, bf16[256,512]{1,0:T(8,128)(2,1)S(1)} %get-tuple-element.31.weights, f32[2,160,128]{2,1,0:T(8,128)S(1)} %collective-permute-done.2.got_low, ...), custom_call_target="tpu_custom_call" | custom-call | tf_op jit(solution)/shard_map/edges/pallas_call | solution.py:417
Async XLA Ops:
  1.1 13.5 %collective-permute-start = (f32[16,16,256]{2,1,0:T(8,128)S(1)}, f32[16,16,256]{2,1,0:T(8,128)S(1)}, u32[]{:S(2)}, u32[]{:S(2)}) collective-permute-start(f32[16,16,256]{2,1,0:T(8,128)S(1)} %get-tuple-element.22), channel_id=1, source_target_pairs={{1,2},{2,1},{3,127},{5,6},{6,5},{7,123},{9,10},{10,9},{11,119},{13... | collective-permute-start | bytes 786440 | tf_op jit(solution)/shard_map/ppermute | solution.py:456
  10.7 3.9 %collective-permute-start.1 = (f32[16,16,256]{2,1,0:T(8,128)S(1)}, f32[16,16,256]{2,1,0:T(8,128)S(1)}, u32[]{:S(2)}, u32[]{:S(2)}) collective-permute-start(f32[16,16,256]{2,1,0:T(8,128)S(1)} %get-tuple-element.23), channel_id=1, source_target_pairs={{0,1},{1,0},{2,3},{3,2},{4,5},{5,4},{6,7},{7,6},{8,9},{9,8},{10,11... | collective-permute-start | bytes 786440 | tf_op jit(solution)/shard_map/ppermute | solution.py:457
  26.9 18.8 %collective-permute-start.2 = (f32[2,160,128]{2,1,0:T(8,128)S(1)}, f32[2,160,128]{2,1,0:T(8,128)S(1)}, u32[]{:S(2)}, u32[]{:S(2)}) collective-permute-start(f32[2,160,128]{2,1,0:T(8,128)S(1)} %get-tuple-element.35), channel_id=1, source_target_pairs={{0,4},{4,8},{8,12},{12,16},{16,20},{20,24},{24,28},{28,32},{32,36}... | collective-permute-start | bytes 491528 | tf_op jit(solution)/shard_map/ppermute | solution.py:462
  28.5 17.3 %collective-permute-start.3 = (f32[2,160,128]{2,1,0:T(8,128)S(1)}, f32[2,160,128]{2,1,0:T(8,128)S(1)}, u32[]{:S(2)}, u32[]{:S(2)}) collective-permute-start(f32[2,160,128]{2,1,0:T(8,128)S(1)} %get-tuple-element.36), channel_id=1, source_target_pairs={{4,0},{8,4},{12,8},{16,12},{20,16},{24,20},{28,24},{32,28},{36,32}... | collective-permute-start | bytes 491528 | tf_op jit(solution)/shard_map/ppermute | solution.py:463

commit v5 on v4

--- a/solution.py
+++ b/solution.py
@@ -20,6 +20,7 @@
 STATE = 4 * K
 PLANES = STATE + K + 1
 VMEM_LIMIT = 24 * 1024 * 1024
+CORE_SPAN = 17
 SPANS = (21, 19, 19, 19, 19, 17, 17, 17)
 
 
@@ -106,7 +107,7 @@
         send_high[group, pl.ds(at, 8)] = high
 
 
-def extend_kernel(x_all, m_all, w_all, tile0, tile1, tile2, send_low, send_high, cor, weights, x, m, w, sems):
+def extend_kernel(x_all, m_all, w_all, tile0, tile1, tile2, send_low, send_high, cor, weights, even0, even1, x, m, w, prod, sems):
     pairs = ((x_all, x), (m_all, m), (w_all, w))
     copies = [pltpu.make_async_copy(a, b, sems.at[i]) for i, (a, b) in enumerate(pairs)]
     for copy in copies:
@@ -136,6 +137,9 @@
 
         place(HALO + r, source, (tile0, tile1, tile2), send_low, send_high)
 
+    early(tile0, cor, (0,), weights, prod, even0)
+    early(tile1, cor, (96,), weights, prod, even1)
+
 
 def halo_rows_kernel(ra, rb, t0, t1, t2, sl, sh, tile0, tile1, tile2, send_low, send_high, folded):
     del t0, t1, t2, sl, sh
@@ -177,10 +181,11 @@
     vmem = pl.BlockSpec(memory_space=pltpu.VMEM)
     tile = jax.ShapeDtypeStruct((PLANES, span + 2 * PAD, LANES), f32)
     send = jax.ShapeDtypeStruct((PLANES // 8, span, LANES), f32)
+    even = jax.ShapeDtypeStruct((STATE, span + 2 * PAD, LANES), f32)
     return pl.pallas_call(
         extend_kernel,
         in_specs=[pl.BlockSpec(memory_space=pltpu.HBM)] * 3,
-        out_specs=[vmem] * 7,
+        out_specs=[vmem] * 9,
         out_shape=[
             tile,
             tile,
@@ -189,11 +194,14 @@
             send,
             jax.ShapeDtypeStruct((span + 2 * PAD, LANES), f32),
             jax.ShapeDtypeStruct((2 * LANES, 4 * LANES), jnp.bfloat16),
+            even,
+            even,
         ],
         scratch_shapes=[
             pltpu.VMEM(x.shape, f32),
             pltpu.VMEM(mixing.shape, f32),
             pltpu.VMEM(land.shape, jnp.int32),
+            pltpu.VMEM((4,) + even.shape, f32),
             pltpu.SemaphoreType.DMA((3,)),
         ],
         compiler_params=params(),
@@ -245,6 +253,56 @@
         got = jnp.dot(both, weights[...], preferred_element_type=jnp.float32)
         for j in range(4 if f < 3 else 3):
             prod[j, planes, rows, :] = got[:, j * LANES : (j + 1) * LANES].reshape(K, count, LANES)
+
+
+def tail_products(src, weights, prod, firsts, count):
+    q = jnp.concatenate([src[pl.ds(0, STATE), pl.ds(f, count), :].reshape(STATE * count, LANES) for f in firsts], axis=0)
+    high = q.astype(jnp.bfloat16)
+    low = (q - high.astype(jnp.float32)).astype(jnp.bfloat16)
+    got = jnp.dot(jnp.concatenate([high, low], axis=1), weights[...], preferred_element_type=jnp.float32)
+    n = STATE * count
+    for i, f in enumerate(firsts):
+        for j in range(4):
+            part = got[i * n : (i + 1) * n, j * LANES : (j + 1) * LANES]
+            prod[j, pl.ds(0, STATE), pl.ds(f, count), :] = part.reshape(STATE, count, LANES)
+
+
+def seam_room(seams):
+    lane = lax.broadcasted_iota(jnp.int32, (8, LANES), 1)
+    room = jnp.full((8, LANES), LANES, jnp.int32)
+    for seam in seams:
+        after = lax.rem(lane - seam + LANES, LANES)
+        room = jnp.minimum(room, jnp.minimum(after, LANES - 1 - after))
+    return room
+
+
+def first_substep(tile, cor, seams, weights, prod, even, pieces):
+    mask = jnp.where(seam_room(seams) >= 2, 1.0, 0.0)
+
+    def put(p, rows, new):
+        even[p, rows, :] = new
+
+    for start, span in pieces:
+
+        def coef(p, t, start=start, span=span):
+            return tile[p, pl.ds(start + t, 8, stride=span), :]
+
+        substep(tile, put, coef, cor, prod, mask, start, start, span)
+
+
+def early(tile, cor, seams, weights, prod, even):
+    first = PAD + HALO
+    block = tile.shape[1] - 2 * first
+    products(tile, weights, prod, first, block)
+    spare = (8 * CORE_SPAN - (block - 4)) // 2
+    first_substep(tile, cor, seams, weights, prod, even, [(first + 2 - spare, CORE_SPAN)])
+
+
+def late(tile, cor, seams, weights, prod, even):
+    south = PAD + 2
+    north = tile.shape[1] - south - HALO
+    tail_products(tile, weights, prod, (south // 8 * 8, north // 8 * 8), HALO + 8)
+    first_substep(tile, cor, seams, weights, prod, even, [(south, 2), (north, 2)])
 
 
 def substep(src, dst, coef, cor, prod, mask, start, dst_start, span, unroll=3):
@@ -316,15 +374,15 @@
     lax.fori_loop(0, span, row, init, unroll=unroll)
 
 
-def window(tile, cor, seams, weights, prod, even, odd, out):
+def window(tile, cor, seams, weights, prod, even, odd, out, started=False):
     span_rows = tile.shape[1] - 2 * PAD
-    lane = lax.broadcasted_iota(jnp.int32, (8, LANES), 1)
-    room = jnp.full((8, LANES), LANES, jnp.int32)
-    for seam in seams:
-        after = lax.rem(lane - seam + LANES, LANES)
-        room = jnp.minimum(room, jnp.minimum(after, LANES - 1 - after))
+    room = seam_room(seams)
     src = tile
     for s in range(STEPS):
+        if s == 0 and started:
+            late(tile, cor, seams, weights, prod, even)
+            src = even
+            continue
         span = SPANS[s]
         need = span_rows - 4 * (s + 1)
         spare = (8 * span - need) // 2
@@ -349,31 +407,36 @@
         src = keep
 
 
-def interior_kernel(seam, tile, cor, weights, out, even, odd, prod):
+def interior_kernel(seam, tile, cor, weights, begun, out, even, odd, prod):
+    del begun
+
     def put(p, rows, new):
         out[p, rows, :] = new
 
-    window(tile, cor, (seam,), weights, prod, even, odd, put)
-
-
-def interior(tile, cor, weights, seam):
+    window(tile, cor, (seam,), weights, prod, even, odd, put, started=True)
+
+
+def interior(tile, cor, weights, begun, seam):
     rows = tile.shape[1]
     block = rows - 2 * PAD - 2 * HALO
     vmem = pl.BlockSpec(memory_space=pltpu.VMEM)
     f32 = jnp.float32
     return pl.pallas_call(
         functools.partial(interior_kernel, seam),
-        in_specs=[vmem] * 3,
-        out_specs=vmem,
-        out_shape=jax.ShapeDtypeStruct((STATE, block + 2 * PAD, LANES), f32),
+        in_specs=[vmem] * 4,
+        out_specs=[vmem, vmem],
+        out_shape=[
+            jax.ShapeDtypeStruct((STATE, block + 2 * PAD, LANES), f32),
+            jax.ShapeDtypeStruct(begun.shape, f32),
+        ],
+        input_output_aliases={3: 1},
         scratch_shapes=[
-            pltpu.VMEM((STATE, rows, LANES), f32),
             pltpu.VMEM((STATE, rows, LANES), f32),
             pltpu.VMEM((4, STATE, rows, LANES), f32),
         ],
         compiler_params=params(),
         name="interior",
-    )(tile, cor, weights)
+    )(tile, cor, weights, begun)[0]
 
 
 def edge_kernel(start, cor, weights, got_low, got_high, inner0, inner1, result, tile, even, odd, prod, out_low, out_high, sems):
@@ -455,13 +518,13 @@
     to_a, to_b = pack_rows(x, mixing, land_sea)
     ra = lax.ppermute(to_a, axes, pairs_a)
     rb = lax.ppermute(to_b, axes, pairs_b)
-    *parts, cor, weights = extend(x, mixing, land_sea)
+    *parts, cor, weights, even0, even1 = extend(x, mixing, land_sea)
     tile0, tile1, tile2, send_low, send_high = halo_rows(ra, rb, *parts)
-    inner0 = interior(tile0, cor, weights, 0)
+    inner0 = interior(tile0, cor, weights, even0, 0)
     send_low, send_high, inner0 = lax.optimization_barrier((send_low, send_high, inner0))
     got_low = lax.ppermute(send_high, "lon", east)
     got_high = lax.ppermute(send_low, "lon", west)
-    inner1 = interior(tile1, cor, weights, 96)
+    inner1 = interior(tile1, cor, weights, even1, 96)
     out = edges(tile2, cor, weights, got_low, got_high, inner0, inner1)
     return out.reshape(ocean_state.shape)
 

time: 59.8 us -> 61.3 us (1.025)
  Pallas kernels: 41.9 us -> 43.9 us
    pallas_call x1, Pallas kernels: 3.39 us -> 6.25 us  [extend(): pl.pallas_call(extend_kernel, in_specs=[pl.BlockSpec(memory_space=pltpu.H...]
    pallas_call x2, Pallas kernels: 22.8 us -> 21.9 us  [interior(): pl.pallas_call(functools.partial(interior_kernel, seam), in_specs=[vmem]...]
  transfers between devices with their start and end apart: 4 -> 4, of which waited for: 1 -> 0; matrix products, arithmetic and copies ran while one was open for 0% -> 0% of each run, Pallas kernels for 25% -> 28%
where the time goes in v5:
time: 61.3 us; the launch traced here: 61.1 us
  Pallas kernels  43.9 us (72%)
  starting transfers between devices  16.9 us (28%)
    pallas_call x2, Pallas kernels, interior(): pl.pallas_call(functools.partial(interior_kernel, seam), in_specs=[vmem]...  21.9 us
    pallas_call x1, Pallas kernels, edges(): pl.pallas_call(edge_kernel, in_specs=[vmem] * 7, out_specs=pl.BlockSpec(m...  13.8 us
    ppermute x1, starting transfers between devices, body(): ra = lax.ppermute(to_a, axes, pairs_a)  9.59 us
    pallas_call x1, Pallas kernels, extend(): pl.pallas_call(extend_kernel, in_specs=[pl.BlockSpec(memory_space=pltpu.H...  6.25 us
    ppermute x1, starting transfers between devices, body(): got_high = lax.ppermute(send_low, 'lon', west)  6.23 us
  transfers between devices with their start and end apart: 4, of which 0 were waited for; matrix products, arithmetic and copies ran while one was open for 0% of the time, Pallas kernels for 28%

profile of v5, /device:TPU:9, one launch (start us, length us, event | category | flops | bytes accessed | tf_op | source)
XLA Modules:
  0.0 61.1 jit_solution(6192581351751722338)
XLA Ops:
  0.0 1.1 %pack_rows.1 = (f32[16,16,256]{2,1,0:T(8,128)S(1)}, f32[16,16,256]{2,1,0:T(8,128)S(1)}) custom-call(f32[12,128,256]{2,1,0:T(8,128)} %bitcast.2, f32[3,128,256]{2,1,0:T(8,128)} %m_all.1, s32[128,256]{1,0:T(8,128)} %w_all.1), custom_call_target="tpu_custom_call" | custom-call | tf_op jit(solution)/shard_map/pack_rows/pallas_call | solution.py:56
  1.1 9.6 %collective-permute-start = (f32[16,16,256]{2,1,0:T(8,128)S(1)}, f32[16,16,256]{2,1,0:T(8,128)S(1)}, u32[]{:S(2)}, u32[]{:S(2)}) collective-permute-start(f32[16,16,256]{2,1,0:T(8,128)S(1)} %get-tuple-element.26), channel_id=1, source_target_pairs={{1,2},{2,1},{3,127},{5,6},{6,5},{7,123},{9,10},{10,9},{11,119},{13... | collective-permute-start | bytes 786440 | tf_op jit(solution)/shard_map/ppermute | solution.py:519
  10.7 0.1 collective-permute-start.1
  10.8 6.2 %extend.1 = (f32[16,176,128]{2,1,0:T(8,128)S(1)}, f32[16,176,128]{2,1,0:T(8,128)S(1)}, f32[16,176,128]{2,1,0:T(8,128)S(1)}, f32[2,160,128]{2,1,0:T(8,128)S(1)}, ...) custom-call(f32[12,128,256]{2,1,0:T(8,128)} %bitcast.3, ...), custom_call_target="tpu_custom_call" | custom-call | tf_op jit(solution)/shard_map/extend/pallas_call | solution.py:185
  17.1 0.0 collective-permute-done.ra
  17.1 0.0 collective-permute-done.1.rb
  17.1 0.9 %halo_rows.1 = (f32[16,176,128]{2,1,0:T(8,128)S(1)}, f32[16,176,128]{2,1,0:T(8,128)S(1)}, f32[16,176,128]{2,1,0:T(8,128)S(1)}, f32[2,160,128]{2,1,0:T(8,128)S(1)}, f32[2,160,128]{2,1,0:T(8,128)S(1)}) custom-call(f32[16,16,256]{2,1,0:T(8,128)S(1)} %collective-permute-done.ra, ...), custom_call_target="tpu_custom_call", output_to_operand_aliasing={{0}: (2, {}), {1}: (3, {}), {2}: (4, {}), {3}: (5, {}), {4}... | custom-call | tf_op jit(solution)/shard_map/halo_rows/pallas_call | solution.py:214
  18.0 11.0 %interior.2 = (f32[12,144,128]{2,1,0:T(8,128)S(1)}, f32[12,176,128]{2,1,0:T(8,128)S(1)}) custom-call(f32[16,176,128]{2,1,0:T(8,128)S(1)} %get-tuple-element.38.tile, f32[176,128]{1,0:T(8,128)S(1)} %get-tuple-element.34.cor, bf16[256,512]{1,0:T(8,128)(2,1)S(1)} %get-tuple-element.35.weights, ...), custom_call_target="tpu_custom_call", output_to_operand_aliasing={{1}: (3, {})} | custom-call | tf_op jit(solution)/shard_map/interior/pallas_call | solution.py:424
  29.0 1.0 %collective-permute-start.2 = (f32[2,160,128]{2,1,0:T(8,128)S(1)}, f32[2,160,128]{2,1,0:T(8,128)S(1)}, u32[]{:S(2)}, u32[]{:S(2)}) collective-permute-start(f32[2,160,128]{2,1,0:T(8,128)S(1)} %get-tuple-element.41), channel_id=1, source_target_pairs={{0,4},{4,8},{8,12},{12,16},{16,20},{20,24},{24,28},{28,32},{32,36}... | collective-permute-start | bytes 491528 | tf_op jit(solution)/shard_map/ppermute | solution.py:525
  30.0 6.2 %collective-permute-start.3 = (f32[2,160,128]{2,1,0:T(8,128)S(1)}, f32[2,160,128]{2,1,0:T(8,128)S(1)}, u32[]{:S(2)}, u32[]{:S(2)}) collective-permute-start(f32[2,160,128]{2,1,0:T(8,128)S(1)} %get-tuple-element.42), channel_id=1, source_target_pairs={{4,0},{8,4},{12,8},{16,12},{20,16},{24,20},{28,24},{32,28},{36,32}... | collective-permute-start | bytes 491528 | tf_op jit(solution)/shard_map/ppermute | solution.py:526
  36.2 11.0 %interior.3 = (f32[12,144,128]{2,1,0:T(8,128)S(1)}, f32[12,176,128]{2,1,0:T(8,128)S(1)}) custom-call(f32[16,176,128]{2,1,0:T(8,128)S(1)} %get-tuple-element.44.tile, f32[176,128]{1,0:T(8,128)S(1)} %get-tuple-element.34.cor, bf16[256,512]{1,0:T(8,128)(2,1)S(1)} %get-tuple-element.35.weights, ...), custom_call_target="tpu_custom_call", output_to_operand_aliasing={{1}: (3, {})} | custom-call | tf_op jit(solution)/shard_map/interior/pallas_call | solution.py:424
  47.2 0.0 collective-permute-done.2.got_low
  47.2 0.0 collective-permute-done.3.got_high
  47.2 13.8 %edges.1 = f32[12,128,256]{2,1,0:T(8,128)} custom-call(f32[16,176,128]{2,1,0:T(8,128)S(1)} %get-tuple-element.33.start, f32[176,128]{1,0:T(8,128)S(1)} %get-tuple-element.34.cor, bf16[256,512]{1,0:T(8,128)(2,1)S(1)} %get-tuple-element.35.weights, f32[2,160,128]{2,1,0:T(8,128)S(1)} %collective-permute-done.2.got_low, ...), custom_call_target="tpu_custom_call" | custom-call | tf_op jit(solution)/shard_map/edges/pallas_call | solution.py:480
Async XLA Ops:
  1.1 16.0 %collective-permute-start = (f32[16,16,256]{2,1,0:T(8,128)S(1)}, f32[16,16,256]{2,1,0:T(8,128)S(1)}, u32[]{:S(2)}, u32[]{:S(2)}) collective-permute-start(f32[16,16,256]{2,1,0:T(8,128)S(1)} %get-tuple-element.26), channel_id=1, source_target_pairs={{1,2},{2,1},{3,127},{5,6},{6,5},{7,123},{9,10},{10,9},{11,119},{13... | collective-permute-start | bytes 786440 | tf_op jit(solution)/shard_map/ppermute | solution.py:519
  10.7 6.4 %collective-permute-start.1 = (f32[16,16,256]{2,1,0:T(8,128)S(1)}, f32[16,16,256]{2,1,0:T(8,128)S(1)}, u32[]{:S(2)}, u32[]{:S(2)}) collective-permute-start(f32[16,16,256]{2,1,0:T(8,128)S(1)} %get-tuple-element.27), channel_id=1, source_target_pairs={{0,1},{1,0},{2,3},{3,2},{4,5},{5,4},{6,7},{7,6},{8,9},{9,8},{10,11... | collective-permute-start | bytes 786440 | tf_op jit(solution)/shard_map/ppermute | solution.py:520
  29.0 18.2 %collective-permute-start.2 = (f32[2,160,128]{2,1,0:T(8,128)S(1)}, f32[2,160,128]{2,1,0:T(8,128)S(1)}, u32[]{:S(2)}, u32[]{:S(2)}) collective-permute-start(f32[2,160,128]{2,1,0:T(8,128)S(1)} %get-tuple-element.41), channel_id=1, source_target_pairs={{0,4},{4,8},{8,12},{12,16},{16,20},{20,24},{24,28},{28,32},{32,36}... | collective-permute-start | bytes 491528 | tf_op jit(solution)/shard_map/ppermute | solution.py:525
  30.0 17.2 %collective-permute-start.3 = (f32[2,160,128]{2,1,0:T(8,128)S(1)}, f32[2,160,128]{2,1,0:T(8,128)S(1)}, u32[]{:S(2)}, u32[]{:S(2)}) collective-permute-start(f32[2,160,128]{2,1,0:T(8,128)S(1)} %get-tuple-element.42), channel_id=1, source_target_pairs={{4,0},{8,4},{12,8},{16,12},{20,16},{24,20},{28,24},{32,28},{36,32}... | collective-permute-start | bytes 491528 | tf_op jit(solution)/shard_map/ppermute | solution.py:526

commit v6 on v4

--- a/solution.py
+++ b/solution.py
@@ -227,8 +227,8 @@
             out = jnp.where(gap == offset % LANES, value, out)
         return out
 
-    east = stencil(((0, 7.0), (1, 7.0), (-1, -1.0), (2, -1.0)))
-    west = stencil(((-1, 7.0), (0, 7.0), (-2, -1.0), (1, -1.0)))
+    east = stencil(((0, 3.5), (1, 3.5), (-1, -0.5), (2, -0.5)))
+    west = stencil(((-1, 3.5), (0, 3.5), (-2, -0.5), (1, -0.5)))
     lap = stencil(((0, -4.0), (1, 1.0), (-1, 1.0)))
     diff = stencil(((1, 1.0), (-1, -1.0)))
     return jnp.concatenate([east, west, lap, diff], axis=1).astype(jnp.bfloat16)
@@ -247,7 +247,7 @@
             prod[j, planes, rows, :] = got[:, j * LANES : (j + 1) * LANES].reshape(K, count, LANES)
 
 
-def substep(src, dst, coef, cor, prod, mask, start, dst_start, span, unroll=3):
+def substep(src, dst, coef, cor, prod, mask, start, dst_start, span, unroll=4):
     def load(ref, p, t):
         return ref[p, pl.ds(start + t, 8, stride=span), :]
 
@@ -255,7 +255,7 @@
         return prod[j, p, pl.ds(start + t, 8, stride=span), :]
 
     def density(t, k):
-        return -0.25 * THERMAL * load(src, k, t) + 0.25 * HALINE * load(src, K + k, t)
+        return load(src, K + k, t) - THERMAL / HALINE * load(src, k, t)
 
     def pressures(t):
         out = [density(t, 0)]
@@ -280,17 +280,18 @@
         below_flux, p_prev, p_here = carry
         wet = coef(STATE + K, t) * mask
         wet24 = wet * (1.0 / 24.0)
+        wet_grad = wet * (0.5 * GRAVITY * HALINE)
         wet_cor = wet * cor[pl.ds(start + t, 8, stride=span), :]
         p_next = pressures(t + 1)
         above = fluxes(t)
         grad_lon = None
         for k in range(K):
             wet_mix = wet * coef(STATE + k, t)
-            drop = -0.25 * THERMAL * line(3, k, t) + 0.25 * HALINE * line(3, K + k, t)
+            drop = line(3, K + k, t) - THERMAL / HALINE * line(3, k, t)
             grad_lon = drop if k == 0 else grad_lon + drop
             u = load(src, 2 * K + k, t)
-            mean = 3.0 * u + 0.5 * line(2, 2 * K + k, t)
-            half = 0.5 * line(3, 2 * K + k, t)
+            mean = 6.0 * u + line(2, 2 * K + k, t)
+            half = line(3, 2 * K + k, t)
             east_speed, west_speed = mean + half, mean - half
             for f in range(4):
                 p = f * K + k
@@ -306,9 +307,9 @@
                         lap = lap + 0.5 * (load(src, p - 1, t) - q)
                 new = q + (wet_mix * lap - wet24 * adv)
                 if f == 2:
-                    new = new + (wet_cor * load(src, p + K, t) - wet * grad_lon)
+                    new = new + (wet_cor * load(src, p + K, t) - wet_grad * grad_lon)
                 if f == 3:
-                    new = new - (wet_cor * load(src, p - K, t) + wet * (p_next[k] - p_prev[k]))
+                    new = new - (wet_cor * load(src, p - K, t) + wet_grad * (p_next[k] - p_prev[k]))
                 dst(p, pl.ds(dst_start + t, 8, stride=span), new)
         return above, p_here, p_next
 

time: 59.8 us -> 59.1 us (0.988)
  no operation moved by 1% of the time
where the time goes in v6:
time: 59.1 us; the launch traced here: 59 us
  Pallas kernels  41.4 us (70%)
  starting transfers between devices  16.9 us (29%)
    pallas_call x2, Pallas kernels, interior(): pl.pallas_call(functools.partial(interior_kernel, seam), in_specs=[vmem]...  22.7 us
    pallas_call x1, Pallas kernels, edges(): pl.pallas_call(edge_kernel, in_specs=[vmem] * 7, out_specs=pl.BlockSpec(m...  13.4 us
    ppermute x1, starting transfers between devices, body(): ra = lax.ppermute(to_a, axes, pairs_a)  9.59 us
    ppermute x1, starting transfers between devices, body(): got_high = lax.ppermute(send_low, 'lon', west)  5.69 us
    pallas_call x1, Pallas kernels, extend(): pl.pallas_call(extend_kernel, in_specs=[pl.BlockSpec(memory_space=pltpu.H...  3.39 us
    ppermute x1, starting transfers between devices, body(): got_low = lax.ppermute(send_high, 'lon', east)  1.57 us
  transfers between devices with their start and end apart: 4, of which 1 were waited for; matrix products, arithmetic and copies ran while one was open for 0% of the time, Pallas kernels for 25%

profile of v6, /device:TPU:9, one launch (start us, length us, event | category | flops | bytes accessed | tf_op | source)
XLA Modules:
  0.0 59.0 jit_solution(3775240098248350013)
XLA Ops:
  0.0 1.1 %pack_rows.1 = (f32[16,16,256]{2,1,0:T(8,128)S(1)}, f32[16,16,256]{2,1,0:T(8,128)S(1)}) custom-call(f32[12,128,256]{2,1,0:T(8,128)} %bitcast.2, f32[3,128,256]{2,1,0:T(8,128)} %m_all.1, s32[128,256]{1,0:T(8,128)} %w_all.1), custom_call_target="tpu_custom_call" | custom-call | tf_op jit(solution)/shard_map/pack_rows/pallas_call | solution.py:55
  1.1 9.6 %collective-permute-start = (f32[16,16,256]{2,1,0:T(8,128)S(1)}, f32[16,16,256]{2,1,0:T(8,128)S(1)}, u32[]{:S(2)}, u32[]{:S(2)}) collective-permute-start(f32[16,16,256]{2,1,0:T(8,128)S(1)} %get-tuple-element.22), channel_id=1, source_target_pairs={{1,2},{2,1},{3,127},{5,6},{6,5},{7,123},{9,10},{10,9},{11,119},{13... | collective-permute-start | bytes 786440 | tf_op jit(solution)/shard_map/ppermute | solution.py:457
  10.7 0.1 collective-permute-start.1
  10.8 3.4 %extend.1 = (f32[16,176,128]{2,1,0:T(8,128)S(1)}, f32[16,176,128]{2,1,0:T(8,128)S(1)}, f32[16,176,128]{2,1,0:T(8,128)S(1)}, f32[2,160,128]{2,1,0:T(8,128)S(1)}, ...) custom-call(f32[12,128,256]{2,1,0:T(8,128)} %bitcast.3, f32[3,128,256]{2,1,0:T(8,128)} %m_all.1, ...), custom_call_target="tpu_custom_call" | custom-call | tf_op jit(solution)/shard_map/extend/pallas_call | solution.py:180
  14.2 0.4 collective-permute-done.ra
  14.6 0.0 collective-permute-done.1.rb
  14.6 0.9 %halo_rows.1 = (f32[16,176,128]{2,1,0:T(8,128)S(1)}, f32[16,176,128]{2,1,0:T(8,128)S(1)}, f32[16,176,128]{2,1,0:T(8,128)S(1)}, f32[2,160,128]{2,1,0:T(8,128)S(1)}, f32[2,160,128]{2,1,0:T(8,128)S(1)}) custom-call(f32[16,16,256]{2,1,0:T(8,128)S(1)} %collective-permute-done.ra, ...), custom_call_target="tpu_custom_call", output_to_operand_aliasing={{0}: (2, {}), {1}: (3, {}), {2}: (4, {}), {3}: (5, {}), {4}... | custom-call | tf_op jit(solution)/shard_map/halo_rows/pallas_call | solution.py:206
  15.5 11.3 %interior.2.inner0 = f32[12,144,128]{2,1,0:T(8,128)S(1)} custom-call(f32[16,176,128]{2,1,0:T(8,128)S(1)} %get-tuple-element.34.tile, f32[176,128]{1,0:T(8,128)S(1)} %get-tuple-element.30.cor, bf16[256,512]{1,0:T(8,128)(2,1)S(1)} %get-tuple-element.31.weights), custom_call_target="tpu_custom_call" | custom-call | tf_op jit(solution)/shard_map/interior/pallas_call | solution.py:365
  26.7 1.6 %collective-permute-start.2 = (f32[2,160,128]{2,1,0:T(8,128)S(1)}, f32[2,160,128]{2,1,0:T(8,128)S(1)}, u32[]{:S(2)}, u32[]{:S(2)}) collective-permute-start(f32[2,160,128]{2,1,0:T(8,128)S(1)} %get-tuple-element.35), channel_id=1, source_target_pairs={{0,4},{4,8},{8,12},{12,16},{16,20},{20,24},{24,28},{28,32},{32,36}... | collective-permute-start | bytes 491528 | tf_op jit(solution)/shard_map/ppermute | solution.py:463
  28.3 5.7 %collective-permute-start.3 = (f32[2,160,128]{2,1,0:T(8,128)S(1)}, f32[2,160,128]{2,1,0:T(8,128)S(1)}, u32[]{:S(2)}, u32[]{:S(2)}) collective-permute-start(f32[2,160,128]{2,1,0:T(8,128)S(1)} %get-tuple-element.36), channel_id=1, source_target_pairs={{4,0},{8,4},{12,8},{16,12},{20,16},{24,20},{28,24},{32,28},{36,32}... | collective-permute-start | bytes 491528 | tf_op jit(solution)/shard_map/ppermute | solution.py:464
  34.0 11.4 %interior.3.inner1 = f32[12,144,128]{2,1,0:T(8,128)S(1)} custom-call(f32[16,176,128]{2,1,0:T(8,128)S(1)} %get-tuple-element.38.tile, f32[176,128]{1,0:T(8,128)S(1)} %get-tuple-element.30.cor, bf16[256,512]{1,0:T(8,128)(2,1)S(1)} %get-tuple-element.31.weights), custom_call_target="tpu_custom_call" | custom-call | tf_op jit(solution)/shard_map/interior/pallas_call | solution.py:365
  45.4 0.0 collective-permute-done.2.got_low
  45.4 0.0 collective-permute-done.3.got_high
  45.4 13.4 %edges.1 = f32[12,128,256]{2,1,0:T(8,128)} custom-call(f32[16,176,128]{2,1,0:T(8,128)S(1)} %get-tuple-element.29.start, f32[176,128]{1,0:T(8,128)S(1)} %get-tuple-element.30.cor, bf16[256,512]{1,0:T(8,128)(2,1)S(1)} %get-tuple-element.31.weights, f32[2,160,128]{2,1,0:T(8,128)S(1)} %collective-permute-done.2.got_low, ...), custom_call_target="tpu_custom_call" | custom-call | tf_op jit(solution)/shard_map/edges/pallas_call | solution.py:418
Async XLA Ops:
  1.1 13.5 %collective-permute-start = (f32[16,16,256]{2,1,0:T(8,128)S(1)}, f32[16,16,256]{2,1,0:T(8,128)S(1)}, u32[]{:S(2)}, u32[]{:S(2)}) collective-permute-start(f32[16,16,256]{2,1,0:T(8,128)S(1)} %get-tuple-element.22), channel_id=1, source_target_pairs={{1,2},{2,1},{3,127},{5,6},{6,5},{7,123},{9,10},{10,9},{11,119},{13... | collective-permute-start | bytes 786440 | tf_op jit(solution)/shard_map/ppermute | solution.py:457
  10.7 3.9 %collective-permute-start.1 = (f32[16,16,256]{2,1,0:T(8,128)S(1)}, f32[16,16,256]{2,1,0:T(8,128)S(1)}, u32[]{:S(2)}, u32[]{:S(2)}) collective-permute-start(f32[16,16,256]{2,1,0:T(8,128)S(1)} %get-tuple-element.23), channel_id=1, source_target_pairs={{0,1},{1,0},{2,3},{3,2},{4,5},{5,4},{6,7},{7,6},{8,9},{9,8},{10,11... | collective-permute-start | bytes 786440 | tf_op jit(solution)/shard_map/ppermute | solution.py:458
  26.7 18.7 %collective-permute-start.2 = (f32[2,160,128]{2,1,0:T(8,128)S(1)}, f32[2,160,128]{2,1,0:T(8,128)S(1)}, u32[]{:S(2)}, u32[]{:S(2)}) collective-permute-start(f32[2,160,128]{2,1,0:T(8,128)S(1)} %get-tuple-element.35), channel_id=1, source_target_pairs={{0,4},{4,8},{8,12},{12,16},{16,20},{20,24},{24,28},{28,32},{32,36}... | collective-permute-start | bytes 491528 | tf_op jit(solution)/shard_map/ppermute | solution.py:463
  28.3 17.1 %collective-permute-start.3 = (f32[2,160,128]{2,1,0:T(8,128)S(1)}, f32[2,160,128]{2,1,0:T(8,128)S(1)}, u32[]{:S(2)}, u32[]{:S(2)}) collective-permute-start(f32[2,160,128]{2,1,0:T(8,128)S(1)} %get-tuple-element.36), channel_id=1, source_target_pairs={{4,0},{8,4},{12,8},{16,12},{20,16},{24,20},{28,24},{32,28},{36,32}... | collective-permute-start | bytes 491528 | tf_op jit(solution)/shard_map/ppermute | solution.py:464
